TPU v7x, 32 devices: a whole 2x2x4 slice. The times are simulated.
32 devices in a mesh: tensor: 4 (over z), context: 4 (over y, core), dp: 2 (over x).
Axes of the slice: x: 2, y: 2, z: 4, core: 2. Of those that a mesh axis runs over, the one named last changes fastest.
Arguments:
- inputs: bfloat16 [2, 3072, 768], P('dp', ('context', 'tensor')), may hold values from -6 to 6
- first_gain: float32 [768], replicated, may hold values from 0.5 to 1.5
- first_shift: float32 [768], replicated, may hold values from -1 to 1
- project_weight: bfloat16 [3, 768, 768], P(None, None, 'tensor'), may hold values from -0.21875 to 0.21875
- project_bias: float32 [2, 768], P(None, 'tensor'), may hold values from -1.5 to 1.5
- attend_weight: bfloat16 [768, 768], P('tensor'), may hold values from -1.25 to 1.25
- attend_bias: float32 [768], replicated, may hold values from -1.5 to 1.5
- second_gain: float32 [768], replicated, may hold values from 0.5 to 1.5
- second_shift: float32 [768], replicated, may hold values from -1 to 1
- expand_weight: bfloat16 [768, 3072], P(None, 'tensor'), may hold values from -0.21875 to 0.21875
- expand_bias: float32 [3072], P('tensor'), may hold values from -1.5 to 1.5
- shrink_weight: bfloat16 [3072, 768], P('tensor'), may hold values from -0.109375 to 0.109375
- shrink_bias: float32 [768], replicated, may hold values from -1.5 to 1.5
- segments: int32 [2, 3072], P('dp'), may hold values from 0 to 15, never falling along the last dimension, each value on 1 to 1536 neighbouring positions
- block_order: int32 [8], replicated, may hold values from 0 to 7, each once
- cotangent: bfloat16 [2, 3072, 768], P('dp', ('context', 'tensor')), may hold values from -6 to 6
Outputs:
- outputs: bfloat16 [2, 3072, 768], P('dp', ('context', 'tensor'))
- grad_inputs: bfloat16 [2, 3072, 768], P('dp', ('context', 'tensor'))
- grad_first_gain: float32 [768], replicated
- grad_first_shift: float32 [768], replicated
- grad_project_weight: float32 [3, 768, 768], P(None, None, 'tensor')
- grad_project_bias: float32 [2, 768], P(None, 'tensor')
- grad_attend_weight: float32 [768, 768], P('tensor')
- grad_attend_bias: float32 [768], replicated
- grad_second_gain: float32 [768], replicated
- grad_second_shift: float32 [768], replicated
- grad_expand_weight: float32 [768, 3072], P(None, 'tensor')
- grad_expand_bias: float32 [3072], P('tensor')
- grad_shrink_weight: float32 [3072, 768], P('tensor')
- grad_shrink_bias: float32 [768], replicated
Inputs may be any that keep to these rules, and one draw needn't show every extreme that they name: `segments`: in each sequence the document numbers never fall; every number appears, each document has 1 to 1536 tokens and one has exactly 1536. Each value appears once: stored block b of 384 tokens holds natural block block_order[b].
All inputs are finite; a program needn't handle non-finite values.
Results may differ from a plain program's by a relative error of at most 0.02.
Values may be sent and summed in bfloat16 or wider, within the bound.
A program may use at most 128 MiB of HBM per device.

v0:
```python
import jax
import jax.numpy as jnp
from jax import lax
from jax.sharding import PartitionSpec as P

HEAD_DIM = 64


NEG_FILL = -1e30
NORM_EPS = 1e-05


def layer_norm(values):
    centre = jnp.mean(values, axis=-1, keepdims=True)
    shifted = values - centre
    spread = jnp.mean(shifted * shifted, axis=-1, keepdims=True)
    return shifted * lax.rsqrt(spread + NORM_EPS)


def affine_norm(values, gain, shift):
    return layer_norm(values) * gain + shift


def gelu_tanh(values):
    return jax.nn.gelu(values, approximate=True)


def stored_places(order, half_rows, seq_len):
    index = jnp.arange(seq_len, dtype=jnp.int32)
    slots = jnp.arange(order.shape[0], dtype=jnp.int32)
    chosen = jnp.sum(
        jnp.where((index // half_rows)[:, None] == slots[None, :], order[None, :], 0), axis=1
    )
    return chosen * half_rows + index % half_rows


def allowed_pairs(query_place, query_seg, key_place, key_seg):
    return (query_seg[:, None] == key_seg[None, :]) & (key_place[None, :] <= query_place[:, None])


def split_heads(values):
    return values.reshape(values.shape[0], -1, HEAD_DIM)


def cross_rows(left, right):
    return lax.dot_general(
        left, right, (((0,), (0,)), ((), ())), preferred_element_type=jnp.float32
    )


def over_blocks(step_fn, running, arrays, size):
    total_rows = arrays[0].shape[0]
    blocks = total_rows // size
    stacked = tuple((item.reshape((blocks, size) + item.shape[1:]) for item in arrays))
    starts = jnp.arange(blocks, dtype=jnp.int32) * size

    def inner(state, element):
        return (step_fn(state, element[0], element[1]), None)

    running, _ = lax.scan(inner, running, (stacked, starts))
    return running


def per_device(
    inputs,
    first_gain,
    first_shift,
    project_weight,
    project_bias,
    attend_weight,
    attend_bias,
    second_gain,
    second_shift,
    expand_weight,
    expand_bias,
    shrink_weight,
    shrink_bias,
    segments,
    block_order,
    cotangent,
):
    own_rows = inputs.shape[1]
    local_width = project_weight.shape[2]
    head_count = local_width // HEAD_DIM
    block_rows = own_rows * lax.axis_size("tensor")
    seq_len = block_rows * lax.axis_size("context")
    half_rows = block_rows // 2
    score_scale = HEAD_DIM ** (-0.5)
    places = stored_places(block_order, half_rows, seq_len)
    seg_stored = jnp.take(segments[0], places)
    my_first = lax.axis_index("context") * block_rows
    query_place = lax.dynamic_slice_in_dim(places, my_first, block_rows)
    query_seg = lax.dynamic_slice_in_dim(seg_stored, my_first, block_rows)
    tokens_own = inputs[0].astype(jnp.float32)
    hidden1 = affine_norm(tokens_own, first_gain, first_shift).astype(jnp.bfloat16)
    hidden1_full = lax.all_gather(hidden1, "tensor", axis=0, tiled=True)
    projected = jnp.einsum(
        "rd,kde->kre", hidden1_full, project_weight, preferred_element_type=jnp.float32
    )
    query_rows = (projected[0] + project_bias[0]).astype(jnp.bfloat16)
    key_rows = projected[1].astype(jnp.bfloat16)
    value_rows = (projected[2] + project_bias[1]).astype(jnp.bfloat16)
    query_heads = split_heads(query_rows)

    def key_mask(key_first, amount):
        key_place = lax.dynamic_slice_in_dim(places, key_first, amount)
        key_seg = lax.dynamic_slice_in_dim(seg_stored, key_first, amount)
        return allowed_pairs(query_place, query_seg, key_place, key_seg)[:, None, :]

    def forward_step(running, pieces, key_first):
        row_max, row_sum, weighted = running
        key_heads = split_heads(pieces[0])
        allowed = key_mask(key_first, pieces[0].shape[0])
        scores = (
            jnp.einsum("qhe,khe->qhk", query_heads, key_heads, preferred_element_type=jnp.float32)
            * score_scale
        )
        scores = jnp.where(allowed, scores, NEG_FILL)
        new_max = jnp.maximum(row_max, jnp.max(scores, axis=-1))
        factor = jnp.exp(row_max - new_max)
        weights = jnp.where(allowed, jnp.exp(scores - new_max[..., None]), 0.0)
        row_sum = row_sum * factor + jnp.sum(weights, axis=-1)
        weighted = weighted * factor[..., None] + jnp.einsum(
            "qhk,khe->qhe",
            weights.astype(jnp.bfloat16),
            split_heads(pieces[1]),
            preferred_element_type=jnp.float32,
        )
        return (new_max, row_sum, weighted)

    start_state = (
        jnp.full((block_rows, head_count), NEG_FILL, jnp.float32),
        jnp.zeros((block_rows, head_count), jnp.float32),
        jnp.zeros((block_rows, head_count, HEAD_DIM), jnp.float32),
    )
    row_max, row_sum, weighted = over_blocks(
        forward_step,
        start_state,
        (
            lax.all_gather(key_rows, "context", axis=0, tiled=True),
            lax.all_gather(value_rows, "context", axis=0, tiled=True),
        ),
        block_rows,
    )
    log_total = row_max + jnp.log(row_sum)
    attended = weighted / row_sum[..., None]
    attended_low = attended.reshape(block_rows, local_width).astype(jnp.bfloat16)
    part = attended_low
    branch = lax.psum_scatter(
        jnp.dot(part, attend_weight, preferred_element_type=jnp.float32).astype(jnp.bfloat16),
        "tensor",
        scatter_dimension=0,
        tiled=True,
    ).astype(jnp.float32)
    middle = tokens_own + branch + attend_bias
    hidden2 = affine_norm(middle, second_gain, second_shift).astype(jnp.bfloat16)
    hidden2_full = lax.all_gather(hidden2, "tensor", axis=0, tiled=True)
    pre_act = jnp.dot(hidden2_full, expand_weight, preferred_element_type=jnp.float32) + expand_bias
    activ = gelu_tanh(pre_act).astype(jnp.bfloat16)
    part = activ
    feed_sum = lax.psum_scatter(
        jnp.dot(part, shrink_weight, preferred_element_type=jnp.float32).astype(jnp.bfloat16),
        "tensor",
        scatter_dimension=0,
        tiled=True,
    ).astype(jnp.float32)
    outputs = (middle + feed_sum + shrink_bias).astype(jnp.bfloat16)[None]
    grad_out = cotangent[0]
    grad_full = lax.all_gather(grad_out, "tensor", axis=0, tiled=True)
    grad_shrink = cross_rows(activ, grad_full)
    grad_shrink_bias = jnp.sum(grad_out.astype(jnp.float32), axis=0)
    grad_act = jnp.dot(grad_full, shrink_weight.T, preferred_element_type=jnp.float32)
    grad_pre = jax.vjp(gelu_tanh, pre_act)[1](grad_act)[0].astype(jnp.bfloat16)
    grad_expand = cross_rows(hidden2_full, grad_pre)
    grad_expand_bias = jnp.sum(grad_pre.astype(jnp.float32), axis=0)
    part = grad_pre
    grad_hidden2 = lax.psum_scatter(
        jnp.dot(part, expand_weight.T, preferred_element_type=jnp.float32).astype(jnp.bfloat16),
        "tensor",
        scatter_dimension=0,
        tiled=True,
    ).astype(jnp.float32)
    second_pull = jax.vjp(affine_norm, middle, second_gain, second_shift)[1]
    grad_middle_norm, grad_second_gain, grad_second_shift = second_pull(grad_hidden2)
    grad_middle = grad_out.astype(jnp.float32) + grad_middle_norm
    grad_middle_low = grad_middle.astype(jnp.bfloat16)
    grad_middle_full = lax.all_gather(grad_middle_low, "tensor", axis=0, tiled=True)
    grad_attend = cross_rows(attended_low, grad_middle_full)
    grad_attend_bias = jnp.sum(grad_middle_low.astype(jnp.float32), axis=0)
    grad_attended = jnp.dot(
        grad_middle_full, attend_weight.T, preferred_element_type=jnp.float32
    ).astype(jnp.bfloat16)
    grad_heads = split_heads(grad_attended)
    delta = jnp.sum(grad_heads.astype(jnp.float32) * attended, axis=-1)

    def probs_for(q_heads, k_heads, lse_rows, allowed):
        scores = (
            jnp.einsum("qhe,khe->qhk", q_heads, k_heads, preferred_element_type=jnp.float32)
            * score_scale
        )
        return jnp.where(allowed, jnp.exp(scores - lse_rows[..., None]), 0.0)

    def grad_scores(weights, out_heads, v_heads, delta_rows):
        grad_weights = jnp.einsum(
            "qhe,khe->qhk", out_heads, v_heads, preferred_element_type=jnp.float32
        )
        return (weights * (grad_weights - delta_rows[..., None])).astype(jnp.bfloat16)

    zero_rows = jnp.zeros((block_rows, head_count, HEAD_DIM), jnp.float32)
    key_all, value_all = (
        lax.all_gather(key_rows, "context", axis=0, tiled=True),
        lax.all_gather(value_rows, "context", axis=0, tiled=True),
    )

    def key_pass(running, key_first):
        key_heads = split_heads(lax.dynamic_slice_in_dim(key_all, key_first, block_rows))
        value_heads = split_heads(lax.dynamic_slice_in_dim(value_all, key_first, block_rows))
        weights = probs_for(query_heads, key_heads, log_total, key_mask(key_first, block_rows))
        score_grad = grad_scores(weights, grad_heads, value_heads, delta)
        running = (
            running
            + jnp.einsum("qhk,khe->qhe", score_grad, key_heads, preferred_element_type=jnp.float32)
            * score_scale
        )
        grad_key = (
            jnp.einsum("qhk,qhe->khe", score_grad, query_heads, preferred_element_type=jnp.float32)
            * score_scale
        )
        grad_value = jnp.einsum(
            "qhk,qhe->khe",
            weights.astype(jnp.bfloat16),
            grad_heads,
            preferred_element_type=jnp.float32,
        )
        return (
            running,
            jnp.concatenate(
                [
                    grad_key.reshape(block_rows, local_width),
                    grad_value.reshape(block_rows, local_width),
                ],
                axis=1,
            ),
        )

    key_starts = jnp.arange(seq_len // block_rows, dtype=jnp.int32) * block_rows
    grad_query, key_terms = lax.scan(key_pass, zero_rows, key_starts)
    key_value_grads = lax.psum_scatter(
        key_terms.reshape(seq_len, 2 * local_width).astype(jnp.bfloat16),
        "context",
        scatter_dimension=0,
        tiled=True,
    ).astype(jnp.float32)
    grad_key = key_value_grads[:, :local_width]
    grad_value = key_value_grads[:, local_width:]
    grad_project_rows = jnp.stack(
        [grad_query.reshape(block_rows, local_width), grad_key, grad_value]
    ).astype(jnp.bfloat16)
    grad_project = jnp.einsum(
        "rd,kre->kde", hidden1_full, grad_project_rows, preferred_element_type=jnp.float32
    )
    grad_project_bias = jnp.stack(
        [
            jnp.sum(grad_project_rows[0].astype(jnp.float32), axis=0),
            jnp.sum(grad_project_rows[2].astype(jnp.float32), axis=0),
        ]
    )
    part = grad_project_rows
    grad_hidden1 = lax.psum_scatter(
        jnp.einsum("kre,kde->rd", part, project_weight, preferred_element_type=jnp.float32).astype(
            jnp.bfloat16
        ),
        "tensor",
        scatter_dimension=0,
        tiled=True,
    ).astype(jnp.float32)
    first_pull = jax.vjp(affine_norm, tokens_own, first_gain, first_shift)[1]
    grad_tokens_norm, grad_first_gain, grad_first_shift = first_pull(grad_hidden1)
    grad_inputs = (grad_middle + grad_tokens_norm).astype(jnp.bfloat16)[None]
    summed = lax.psum(
        (grad_project, grad_project_bias, grad_attend, grad_expand, grad_expand_bias, grad_shrink),
        ("context", "dp"),
    )
    vectors = lax.psum(
        (
            grad_first_gain,
            grad_first_shift,
            grad_attend_bias,
            grad_second_gain,
            grad_second_shift,
            grad_shrink_bias,
        ),
        ("tensor", "context", "dp"),
    )
    return (
        outputs,
        grad_inputs,
        vectors[0],
        vectors[1],
        summed[0],
        summed[1],
        summed[2],
        vectors[2],
        vectors[3],
        vectors[4],
        summed[3],
        summed[4],
        summed[5],
        vectors[5],
    )


def solution(mesh):
    in_specs = (
        P("dp", ("context", "tensor"), None),
        P(),
        P(),
        P(None, None, "tensor"),
        P(None, "tensor"),
        P("tensor", None),
        P(),
        P(),
        P(),
        P(None, "tensor"),
        P("tensor"),
        P("tensor", None),
        P(),
        P("dp", None),
        P(),
        P("dp", ("context", "tensor"), None),
    )
    out_specs = (
        P("dp", ("context", "tensor"), None),
        P("dp", ("context", "tensor"), None),
        P(),
        P(),
        P(None, None, "tensor"),
        P(None, "tensor"),
        P("tensor", None),
        P(),
        P(),
        P(),
        P(None, "tensor"),
        P("tensor"),
        P("tensor", None),
        P(),
    )
    return jax.shard_map(
        per_device, mesh=mesh, in_specs=in_specs, out_specs=out_specs, check_vma=False
    )
```

profile of v0, /device:TPU:0, one launch (start us, length us, event | category | flops | bytes accessed | tf_op | source)
XLA Modules:
  0.0 606.1 jit_solution(4479381773742738639)
XLA Ops:
  10.8 1.9 fusion.54
  12.8 33.1 %all-gather.9.cloned.1.call-done = bf16[768,768]{1,0:T(8,128)(2,1)} async-done(((bf16[192,768]{1,0:T(8,128)(2,1)}), bf16[768,768]{1,0:T(8,128)(2,1)}) %all-gather.9.cloned.1.call-update) | async-done | bytes 1179664 | tf_op jit(solution)/shard_map/all_gather | solution.py:96
  45.9 2.4 fusion.88
  50.5 1.9 fusion.63
  52.7 17.4 %gather_fusion = s32[3072]{0:T(1024)S(1)} fusion(s32[3072]{0:T(1024)S(1)} %bitcast.270, s32[3072]{0:T(1024)S(1)} %broadcast_clamp_fusion), kind=kCustom, calls=%fused_computation | custom fusion | bytes 36864 | tf_op jit(solution)/shard_map/jit(_take)/gather | solution.py:90
  71.5 1.4 dynamic_slice.38
  74.6 3.5 reshape.298
  78.1 1.4 copy.48
  79.5 7.2 %all-gather.11.cloned.1.call-done = bf16[3072,192]{0,1:T(8,128)(2,1)} async-done(((bf16[768,192]{0,1:T(8,128)(2,1)}), bf16[3072,192]{0,1:T(8,128)(2,1)}) %all-gather.11.cloned.1.call-update) | async-done | bytes 1179664 | tf_op jit(solution)/shard_map/all_gather | solution.py:141
  86.7 2.4 copy.58
  89.1 54.7 %while.28 = (s32[]{:T(128)}, f32[768,3]{0,1:T(4,128)S(1)}, f32[768,3]{0,1:T(4,128)}, f32[768,3,64]{0,2,1:T(8,128)S(1)}, s32[768]{0:T(1024)}, /*index=5*/s32[4]{0...) while((s32[]{:T(128)}, f32[768,3]{0,1:T(4,128)S(1)}, ...), condition=%wide.region_6.7_spmd.clone, body=%wide.region_3.6_spmd.clone.sunk | while | flops 478211328 | bytes 27009240 | solution.py:60
  96.0 1.5 fusion.148
  97.5 1.8 fusion.149
  99.9 2.3 fusion.151
  109.2 1.5 fusion.148
  110.7 1.8 fusion.149
  113.8 2.3 fusion.151
  123.0 1.5 fusion.148
  124.6 1.8 fusion.149
  127.7 2.3 fusion.151
  136.9 1.5 fusion.148
  138.4 1.8 fusion.149
  141.5 2.3 fusion.151
  144.6 2.5 convolution_convert_fusion.2
  147.2 29.4 %reduce-scatter.6.cloned.1.call-done = bf16[192,768]{1,0:T(8,128)(2,1)} async-done(((bf16[768,768]{1,0:T(8,128)(2,1)}), bf16[192,768]{1,0:T(8,128)(2,1)}) %reduce-scatter.6.cloned.1.call-update) | async-done | bytes 294928 | tf_op jit(solution)/shard_map/reduce_scatter | solution.py:149
  179.0 1.9 add_convert_fusion.2
  181.8 28.2 %all-gather.13.cloned.1.call-done = bf16[768,768]{1,0:T(8,128)(2,1)} async-done(((bf16[192,768]{1,0:T(8,128)(2,1)}), bf16[768,768]{1,0:T(8,128)(2,1)}) %all-gather.13.cloned.1.call-update) | async-done | bytes 1179664 | tf_op jit(solution)/shard_map/all_gather | solution.py:157
  209.9 4.1 fusion.89
  214.1 26.8 %all-gather.19.cloned.1.call-done = bf16[1,768,768]{2,1,0:T(8,128)(2,1)} async-done(((bf16[1,192,768]{2,1,0:T(8,128)(2,1)}), bf16[1,768,768]{2,1,0:T(8,128)(2,1)}) %all-gather.19.cloned.1.call-update) | async-done | bytes 1179664 | tf_op jit(solution)/shard_map/all_gather | solution.py:169
  240.9 5.0 convert_reduce_fusion
  246.9 2.1 convolution_convert_fusion
  249.2 4.3 convolution_convert_fusion.1
  253.6 24.3 %reduce-scatter.10.cloned.1.call-done = bf16[192,768]{1,0:T(8,128)(2,1)} async-done(((bf16[768,768]{1,0:T(8,128)(2,1)}), bf16[192,768]{1,0:T(8,128)(2,1)}) %reduce-scatter.10.cloned.1.call-update) | async-done | bytes 294928 | tf_op jit(solution)/shard_map/reduce_scatter | solution.py:177
  277.8 1.9 fusion.60
  280.4 28.2 %reduce-scatter.8.cloned.1.call-done = bf16[192,768]{1,0:T(8,128)(2,1)} async-done(((bf16[768,768]{1,0:T(8,128)(2,1)}), bf16[192,768]{1,0:T(8,128)(2,1)}) %reduce-scatter.8.cloned.1.call-update) | async-done | bytes 294928 | tf_op jit(solution)/shard_map/reduce_scatter | solution.py:161
  308.7 2.2 fusion.85
  310.8 1.5 convert_reduce_fusion.5
  313.9 27.4 %all-gather.15.cloned.1.call-done = bf16[768,768]{1,0:T(8,128)(2,1)} async-done(((bf16[192,768]{1,0:T(8,128)(2,1)}), bf16[768,768]{1,0:T(8,128)(2,1)}) %all-gather.15.cloned.1.call-update) | async-done | bytes 1179664 | tf_op jit(solution)/shard_map/all_gather | solution.py:187
  341.4 1.8 convolution_convert_fusion.3
  344.0 62.4 %while.29 = (s32[]{:T(128)}, f32[768,3,64]{0,2,1:T(8,128)S(1)}, bf16[4,768,384]{1,2,0:T(8,128)(2,1)}, s32[4]{0:T(128)}, bf16[3072,192]{0,1:T(8,128)(2,1)}, /*ind...) while((s32[]{:T(128)}, f32[768,3,64]{0,2,1:T(8,128)S(1)}, ...), condition=%wide.region_16.17_spmd.clone, body=%wide.region_15.16_spmd.clone.sunk | while | flops 1153843200 | bytes 39902472 | solution.py:247
  349.9 1.3 constant_dynamic-slice_fusion.7
  352.4 1.7 fusion.165
  354.1 2.7 fusion.163
  368.0 1.7 fusion.165
  369.7 2.7 fusion.163
  383.6 1.7 fusion.165
  385.3 2.7 fusion.163
  399.2 1.7 fusion.165
  400.9 2.7 fusion.163
  406.4 3.4 copy.56
  409.9 32.1 %reduce-scatter.12.cloned.1.call-done = bf16[768,384]{0,1:T(8,128)(2,1)} async-done(((bf16[3072,384]{0,1:T(8,128)(2,1)}), bf16[768,384]{0,1:T(8,128)(2,1)}) %reduce-scatter.12.cloned.1.call-update) | async-done | bytes 589840 | tf_op jit(solution)/shard_map/reduce_scatter | solution.py:248
  443.1 2.3 bitcast_convert_fusion
  445.5 4.3 fusion.91
  449.8 2.8 fusion.37
  453.9 2.1 convolution_bitcast_fusion
  457.2 14.7 %all-reduce.1 = (f32[2,192]{1,0:T(2,128)}, f32[768]{0:T(1024)}) all-reduce(f32[2,192]{1,0:T(2,128)S(1)} %pad_maximum_fusion.3, f32[768]{0:T(1024)S(1)} %copy-done.32), channel_id=1, replica_groups=mesh['tensor'=4,'context'=4,'dp'=2] {'context','dp'}, use_global_device_ids=true, to_apply=%region_28.29 | all-reduce | flops 1152 | bytes 9216 | tf_op jit(solution)/shard_map/psum | solution.py:280
  471.9 3.0 reduce-scatter.14.cloned.1.call-done
  476.2 1.4 fusion.61
  477.5 40.2 %all-reduce = (f32[768]{0:T(1024)}, f32[768]{0:T(1024)}, f32[768]{0:T(1024)}, f32[768]{0:T(1024)}, f32[768]{0:T(1024)}, /*index=5*/f32[768]{0:T(1024)}) all-reduce(f32[768]{0:T(1024)S(1)} %get-tuple-element.278, f32[768]{0:T(1024)S(1)} %get-tuple-element.281, ...), channel_id=1, replica_groups=mesh['tensor'=4,'context'=4,'dp'=2] {'tensor','context','dp'}, use_global_device_ids=true, to_apply=%region_22.23 | all-reduce | flops 4608 | bytes 36864 | tf_op jit(solution)/shard_map/psum | solution.py:284
  517.7 2.0 fusion.69
  519.7 71.8 %all-reduce.5.cloned.1.call-done = (f32[3,768,192]{1,2,0:T(8,128)}, f32[192,768]{1,0:T(8,128)}, f32[768,768]{1,0:T(8,128)}, f32[768,768]{1,0:T(8,128)}) async-done(((f32[3,768,192]{1,2,0:T(8,128)}, f32[192,768]{1,0:T(8,128)}, f32[768,768]{1,0:T(8,128)}, f32[768,768]{1,0:T(8,128)}), (f32[3,768,192]{1,2,0:T(8,128)}, f32[192,768]{1,0:T(8,128)}, f32[768,768]{1,0:T(8,128)}, ...) | async-done | bytes 7077904 | tf_op jit(solution)/shard_map/psum | solution.py:280
  591.5 2.9 copy.85
  595.3 1.4 copy.87
  597.8 1.4 copy.88
  (226 shorter events, 84.3 us)
Async XLA Ops:
  7.2 233.7 %copy-start = (bf16[768,768]{1,0:T(8,128)(2,1)S(1)}, bf16[768,768]{1,0:T(8,128)(2,1)}, u32[]{:S(2)}) copy-start(bf16[768,768]{1,0:T(8,128)(2,1)} %param.31) | copy-start | bytes 3538948
  7.2 38.7 %all-gather.9.cloned.1.call-start = ((), (), s32[]{:S(2)}) async-start(), calls=%async_computation.5 | async-start | bytes 1474560 | tf_op jit(solution)/shard_map/all_gather | solution.py:96
  8.4 1.8 copy-start.16
  9.6 0.6 copy-start.26
  10.2 0.6 copy-start.19
  12.7 61.9 %all-gather.17.cloned.1.call-start = ((), (), s32[]{:S(2)}) async-start(), calls=%async_computation.14 | async-start | bytes 1474560 | tf_op jit(solution)/shard_map/all_gather | solution.py:140
  45.9 4.5 copy-start.33
  45.9 6.6 %copy-start.34 = (s32[8]{0:T(128)S(1)}, s32[8]{0:T(128)}, u32[]{:S(2)}) copy-start(s32[8]{0:T(128)} %param.34) | copy-start | bytes 100
  48.3 1.2 copy-start.10
  48.3 4.3 copy-start.2
  50.3 36.4 %all-gather.11.cloned.1.call-start = ((), (), s32[]{:S(2)}) async-start(), calls=%async_computation.6 | async-start | bytes 1474560 | tf_op jit(solution)/shard_map/all_gather | solution.py:141
  52.4 124.3 %reduce-scatter.6.cloned.1.call-start = ((), (), s32[]{:S(2)}) async-start(), calls=%async_computation.7 | async-start | bytes 1474560 | tf_op jit(solution)/shard_map/reduce_scatter | solution.py:149
  143.8 32.8 %copy-start.3 = (bf16[1,192,768]{2,1,0:T(8,128)(2,1)S(1)}, bf16[1,192,768]{2,1,0:T(8,128)(2,1)}, u32[]{:S(2)}) copy-start(bf16[1,192,768]{2,1,0:T(8,128)(2,1)} %param.20) | copy-start | bytes 884740
  143.8 32.8 %copy-start.13 = (f32[768]{0:T(1024)S(1)}, f32[768]{0:T(1024)}, u32[]{:S(2)}) copy-start(f32[768]{0:T(1024)} %param.26) | copy-start | bytes 9220
  143.8 35.2 %copy-start.15 = (f32[768]{0:T(1024)S(1)}, f32[768]{0:T(1024)}, u32[]{:S(2)}) copy-start(f32[768]{0:T(1024)} %param.27) | copy-start | bytes 9220
  143.8 35.2 %copy-start.31 = (f32[768]{0:T(1024)S(1)}, f32[768]{0:T(1024)}, u32[]{:S(2)}) copy-start(f32[768]{0:T(1024)} %param.28) | copy-start | bytes 9220
  147.2 62.8 %all-gather.13.cloned.1.call-start = ((), (), s32[]{:S(2)}) async-start(), calls=%async_computation.8 | async-start | bytes 1474560 | tf_op jit(solution)/shard_map/all_gather | solution.py:157
  177.8 36.2 %copy-start.18 = (f32[192]{0:T(256)}, f32[192]{0:T(256)S(1)}, u32[]{:S(2)}) copy-start(f32[192]{0:T(256)S(1)} %broadcast_multiply_fusion.1) | copy-start | bytes 2308
  179.0 35.1 %copy-start.28 = (f32[192]{0:T(256)}, f32[192]{0:T(256)S(1)}, u32[]{:S(2)}) copy-start(f32[192]{0:T(256)S(1)} %multiply_reduce_fusion.1) | copy-start | bytes 2308
  179.0 35.0 %copy-start.24 = (f32[192]{0:T(256)}, f32[192]{0:T(256)S(1)}, u32[]{:S(2)}) copy-start(f32[192]{0:T(256)S(1)} %fusion.81) | copy-start | bytes 2308
  180.9 59.9 %all-gather.19.cloned.1.call-start = ((), (), s32[]{:S(2)}) async-start(), calls=%async_computation.15 | async-start | bytes 1474560 | tf_op jit(solution)/shard_map/all_gather | solution.py:169
  181.5 59.4 %copy-start.39 = (f32[768]{0:T(1024)S(1)}, f32[768]{0:T(1024)}, u32[]{:S(2)}) copy-start(f32[768]{0:T(1024)} %param.30) | copy-start | bytes 9220
  181.5 96.3 %reduce-scatter.10.cloned.1.call-start = ((), (), s32[]{:S(2)}) async-start(), calls=%async_computation.10 | async-start | bytes 1474560 | tf_op jit(solution)/shard_map/reduce_scatter | solution.py:177
  240.9 6.1 %copy-start.35 = (bf16[768,768]{1,0:T(8,128)(2,1)S(1)}, bf16[768,768]{1,0:T(8,128)(2,1)}, u32[]{:S(2)}) copy-start(bf16[768,768]{1,0:T(8,128)(2,1)} %param.29) | copy-start | bytes 3538948
  245.9 1.0 copy-start.42
  249.1 28.7 %copy-start.4 = (bf16[192,768]{1,0:T(8,128)(2,1)S(1)}, bf16[192,768]{1,0:T(8,128)(2,1)}, u32[]{:S(2)}) copy-start(bf16[192,768]{1,0:T(8,128)(2,1)} %reduce-scatter.6.cloned.1.call-done) | copy-start | bytes 884740
  249.1 59.6 %reduce-scatter.8.cloned.1.call-start = ((), (), s32[]{:S(2)}) async-start(), calls=%async_computation.9 | async-start | bytes 1474560 | tf_op jit(solution)/shard_map/reduce_scatter | solution.py:161
  253.5 57.4 %copy-start.6 = (bf16[1,192,768]{2,1,0:T(8,128)(2,1)S(1)}, bf16[1,192,768]{2,1,0:T(8,128)(2,1)}, u32[]{:S(2)}) copy-start(bf16[1,192,768]{2,1,0:T(8,128)(2,1)} %param.35) | copy-start | bytes 884740
  253.5 87.8 %copy-start.11 = (bf16[192,768]{1,0:T(8,128)(2,1)S(1)}, bf16[192,768]{1,0:T(8,128)(2,1)}, u32[]{:S(2)}) copy-start(bf16[192,768]{1,0:T(8,128)(2,1)} %param.25) | copy-start | bytes 884740
  253.5 87.8 %all-gather.15.cloned.1.call-start = ((), (), s32[]{:S(2)}) async-start(), calls=%async_computation.11 | async-start | bytes 1474560 | tf_op jit(solution)/shard_map/all_gather | solution.py:187
  310.8 3.1 copy-start.29
  312.3 129.7 %reduce-scatter.12.cloned.1.call-start = ((), (), s32[]{:S(2)}) async-start(), calls=%async_computation.12 | async-start | bytes 2949120 | tf_op jit(solution)/shard_map/reduce_scatter | solution.py:248
  351.3 1.1 copy-start.25
  366.9 1.1 copy-start.25
  382.5 1.1 copy-start.25
  398.0 1.1 copy-start.25
  409.8 33.3 %copy-start.38 = (bf16[3,768,192]{1,2,0:T(8,128)(2,1)S(1)}, bf16[3,768,192]{1,2,0:T(8,128)(2,1)}, u32[]{:S(2)}) copy-start(bf16[3,768,192]{1,2,0:T(8,128)(2,1)} %param.23) | copy-start | bytes 2654212
  409.8 65.0 %reduce-scatter.14.cloned.1.call-start = ((), (), s32[]{:S(2)}) async-start(), calls=%async_computation.13 | async-start | bytes 1474560 | tf_op jit(solution)/shard_map/reduce_scatter | solution.py:269
  445.4 4.4 copy-start.40
  445.4 146.1 %all-reduce.5.cloned.1.call-start = ((), (), s32[]{:S(2)}) async-start(), calls=%async_computation.16 | async-start | bytes 14155776 | tf_op jit(solution)/shard_map/psum | solution.py:280
  445.5 4.3 copy-start.37
  445.5 4.3 copy-start.41
  449.8 2.9 copy-start.5
  449.8 4.1 copy-start.36
  456.0 1.1 copy-start.9
  456.0 1.2 copy-start.32
  456.0 18.9 %copy-start.14 = (f32[768]{0:T(1024)S(1)}, f32[768]{0:T(1024)}, u32[]{:S(2)}) copy-start(f32[768]{0:T(1024)} %param.21) | copy-start | bytes 9220
  456.0 18.9 %copy-start.17 = (f32[192]{0:T(256)S(1)}, f32[192]{0:T(256)}, u32[]{:S(2)}) copy-start(f32[192]{0:T(256)} %copy-done.16) | copy-start | bytes 2308
  456.0 20.1 %copy-start.27 = (f32[192]{0:T(256)S(1)}, f32[192]{0:T(256)}, u32[]{:S(2)}) copy-start(f32[192]{0:T(256)} %copy-done.26) | copy-start | bytes 2308
  456.0 20.2 %copy-start.20 = (f32[192]{0:T(256)S(1)}, f32[192]{0:T(256)}, u32[]{:S(2)}) copy-start(f32[192]{0:T(256)} %copy-done.19) | copy-start | bytes 2308
  456.0 21.5 %copy-start.21 = (f32[768]{0:T(1024)S(1)}, f32[768]{0:T(1024)}, u32[]{:S(2)}) copy-start(f32[768]{0:T(1024)} %get-tuple-element.276) | copy-start | bytes 9220
  456.0 21.5 %copy-start.22 = (f32[768]{0:T(1024)S(1)}, f32[768]{0:T(1024)}, u32[]{:S(2)}) copy-start(f32[768]{0:T(1024)} %get-tuple-element.280) | copy-start | bytes 9220
  456.0 21.5 %copy-start.23 = (f32[768]{0:T(1024)S(1)}, f32[768]{0:T(1024)}, u32[]{:S(2)}) copy-start(f32[768]{0:T(1024)} %get-tuple-element.349) | copy-start | bytes 9220
  456.0 61.7 %copy-start.30 = (f32[192]{0:T(256)S(1)}, f32[192]{0:T(256)}, u32[]{:S(2)}) copy-start(f32[192]{0:T(256)} %copy-done.29) | copy-start | bytes 2308
  591.5 3.0 copy-start.12
  591.5 3.8 copy-start.8
  595.3 2.5 copy-start.7
  595.3 3.9 copy-start.1
Sparse Core Ops, SparseCore 0:
  12.8 32.9 all-gather.8
  50.4 16.6 all-gather.16
  69.2 17.4 all-gather.10
  147.3 29.3 reduce-scatter.5
  181.1 28.8 all-gather.12
  211.4 29.4 all-gather.18
  249.2 28.5 reduce-scatter.9
  280.7 27.9 reduce-scatter.7
  312.5 28.8 all-gather.14
  410.0 32.0 reduce-scatter.11
  445.5 29.3 reduce-scatter.13
  479.6 111.9 all-reduce.4
where the time goes:
time: 609 us; the launch traced here: 606 us
  waiting for transfers between devices  312 us (51%)
  matrix products  80 us (13%)
  local copies, waits for them, and re-layouts  76.5 us (13%)
  blocking collectives  54.9 us (9%)
  other arithmetic  50.8 us (8%)
  loops' own time  16 us (3%)
  between operations  14.8 us (2%)
    psum x1, waiting for transfers between devices, per_device(): lax.psum((grad_project, grad_project_bias, grad_attend, grad_expand, grad...  71.8 us
    psum x1, blocking collectives, per_device(): lax.psum((grad_first_gain, grad_first_shift, grad_attend_bias, grad_secon...  40.2 us
    all_gather x1, waiting for transfers between devices, per_device(): hidden1_full = lax.all_gather(hidden1, 'tensor', axis=0, tiled=True)  33.1 us
    reduce_scatter x1, waiting for transfers between devices, per_device(): lax.psum_scatter(key_terms.reshape(seq_len, 2 * local_width).astype(jnp.b...  32.1 us
    reduce_scatter x1, waiting for transfers between devices, per_device(): lax.psum_scatter(jnp.dot(part, attend_weight, preferred_element_type=jnp....  29.4 us
    reduce_scatter x1, waiting for transfers between devices, per_device(): lax.psum_scatter(jnp.dot(part, shrink_weight, preferred_element_type=jnp....  28.2 us
    all_gather x1, waiting for transfers between devices, per_device(): hidden2_full = lax.all_gather(hidden2, 'tensor', axis=0, tiled=True)  28.2 us
    all_gather x1, waiting for transfers between devices, per_device(): lax.all_gather(grad_middle_low, 'tensor', axis=0, tiled=True)  27.4 us
  transfers between devices with their start and end apart: 12, of which 11 were waited for; matrix products, arithmetic and copies ran while one was open for 9% of the time, Pallas kernels for 0%

commit v1 on v0

v1 whole, which is shorter than its diff:
```python
import functools

import jax
import jax.numpy as jnp
from jax import lax
from jax.experimental import pallas as pl
from jax.experimental.pallas import tpu as pltpu
from jax.sharding import PartitionSpec as P

HEAD_DIM = 64
NEG_FILL = -1e30
NORM_EPS = 1e-05
DOC_LIMIT = 16
MESH = pl.DeviceIdType.MESH
VM = pl.BlockSpec(memory_space=pltpu.VMEM)
SM = pl.BlockSpec(memory_space=pltpu.SMEM)
DMA = pltpu.SemaphoreType.DMA


def remote_params(collective_id):
    return pltpu.CompilerParams(
        collective_id=collective_id, has_side_effects=True, vmem_limit_bytes=48 << 20
    )


def line_barrier(me, n):
    bar = pltpu.get_barrier_semaphore()

    @pl.when(me > 0)
    def _():
        pl.semaphore_signal(bar, inc=1, device_id={"tensor": me - 1}, device_id_type=MESH)

    @pl.when(me < n - 1)
    def _():
        pl.semaphore_signal(bar, inc=1, device_id={"tensor": me + 1}, device_id_type=MESH)

    pl.semaphore_wait(bar, jnp.where(me > 0, 1, 0) + jnp.where(me < n - 1, 1, 0))


def gather_kernel(n, x_ref, o_ref, send, recv, loc):
    me = lax.axis_index("tensor")
    line_barrier(me, n)
    own = pltpu.make_async_copy(x_ref, o_ref.at[me], loc)
    own.start()

    def copy(d, s):
        shard = jnp.clip(me - s if d == 0 else me + s, 0, n - 1)
        return pltpu.make_async_remote_copy(
            src_ref=x_ref if s == 0 else o_ref.at[shard],
            dst_ref=o_ref.at[shard],
            send_sem=send.at[d, s],
            recv_sem=recv.at[d, s],
            device_id={"tensor": jnp.clip(me + 1 if d == 0 else me - 1, 0, n - 1)},
            device_id_type=MESH,
        )

    def sends(d, s):
        return (me - s >= 0) & (me < n - 1) if d == 0 else (me + s < n) & (me > 0)

    def gets(d, s):
        return me - 1 - s >= 0 if d == 0 else me + 1 + s < n

    def landed(d, s):
        shard = jnp.clip(me - 1 - s if d == 0 else me + 1 + s, 0, n - 1)
        return pltpu.make_async_copy(o_ref.at[shard], o_ref.at[shard], recv.at[d, s])

    for s in range(n - 1):
        for d in range(2):
            if s > 0:

                @pl.when(gets(d, s - 1))
                def _():
                    landed(d, s - 1).wait()

            @pl.when(sends(d, s))
            def _():
                copy(d, s).start()

    for d in range(2):

        @pl.when(gets(d, n - 2))
        def _():
            landed(d, n - 2).wait()

        for s in range(n - 1):

            @pl.when(sends(d, s))
            def _():
                copy(d, s).wait_send()

    own.wait()


def gather_rows(x, n, collective_id):
    rows, cols = x.shape
    return pl.pallas_call(
        functools.partial(gather_kernel, n),
        out_shape=jax.ShapeDtypeStruct((n, rows, cols), x.dtype),
        in_specs=[VM],
        out_specs=VM,
        scratch_shapes=[DMA((2, n - 1)), DMA((2, n - 1)), DMA],
        compiler_params=remote_params(collective_id),
    )(x).reshape(n * rows, cols)


def scatter_kernel(n, x_ref, o_ref, buf, tmp, send, recv):
    me = lax.axis_index("tensor")
    line_barrier(me, n)

    def term(d, k):
        return n - 1 - k if d == 0 else k

    def sends(d, k):
        return me < n - 1 - k if d == 0 else me > k

    def behind(d):
        return me > 0 if d == 0 else me < n - 1

    def copy(d, k, first):
        return pltpu.make_async_remote_copy(
            src_ref=x_ref.at[term(d, k)] if first else tmp.at[d, k],
            dst_ref=buf.at[d, k],
            send_sem=send.at[d, k],
            recv_sem=recv.at[d, k],
            device_id={"tensor": jnp.clip(me + 1 if d == 0 else me - 1, 0, n - 1)},
            device_id_type=MESH,
        )

    def landed(d, k):
        return pltpu.make_async_copy(buf.at[d, k], buf.at[d, k], recv.at[d, k])

    for d in range(2):

        @pl.when(jnp.logical_not(behind(d)))
        def _():
            for k in range(n - 1):
                copy(d, k, True).start()

    for k in range(n - 1):
        for d in range(2):

            @pl.when(behind(d) & sends(d, k))
            def _():
                landed(d, k).wait()
                both = buf[d, k].astype(jnp.float32) + x_ref[term(d, k)].astype(jnp.float32)
                tmp[d, k] = both.astype(tmp.dtype)
                copy(d, k, False).start()

    o_ref[...] = x_ref[me].astype(jnp.float32)
    for d in range(2):
        for k in range(n - 1):

            @pl.when(behind(d) & (me == term(d, k)))
            def _():
                landed(d, k).wait()
                o_ref[...] += buf[d, k].astype(jnp.float32)

    for d in range(2):
        for k in range(n - 1):

            @pl.when(sends(d, k))
            def _():
                copy(d, k, False).wait_send()


def scatter_rows(x, n, collective_id):
    rows, cols = x.shape
    own = rows // n
    return pl.pallas_call(
        functools.partial(scatter_kernel, n),
        out_shape=jax.ShapeDtypeStruct((own, cols), jnp.float32),
        in_specs=[VM],
        out_specs=VM,
        scratch_shapes=[
            pltpu.VMEM((2, n - 1, own, cols), x.dtype),
            pltpu.VMEM((2, n - 1, own, cols), x.dtype),
            DMA((2, n - 1)),
            DMA((2, n - 1)),
        ],
        compiler_params=remote_params(collective_id),
    )(x.reshape(n, own, cols))


def group_barrier(axes, sizes):
    mine = [lax.axis_index(name) for name in axes]
    place = sum_index(mine, sizes)
    total = 1
    for size in sizes:
        total *= size
    bar = pltpu.get_barrier_semaphore()
    for shift in range(1, total):
        other = lax.rem(place + shift, total)
        pl.semaphore_signal(bar, inc=1, device_id=spread(other, axes, sizes), device_id_type=MESH)
    pl.semaphore_wait(bar, total - 1)
    return place, total


def sum_index(mine, sizes):
    place = 0
    for at, size in zip(mine, sizes):
        place = place * size + at
    return place


def spread(place, axes, sizes):
    found = {}
    for name, size in reversed(tuple(zip(axes, sizes))):
        found[name] = lax.rem(place, size)
        place = lax.div(place, size)
    return found


def to_heads_kernel(nc, heads, x_ref, o_ref, send, recv, loc):
    me, _ = group_barrier(("context",), (nc,))

    def copy(shift):
        other = lax.rem(me + shift, nc)
        return other, pltpu.make_async_remote_copy(
            src_ref=x_ref.at[jnp.minimum(other, heads - 1)],
            dst_ref=o_ref.at[me],
            send_sem=send.at[shift],
            recv_sem=recv.at[shift],
            device_id={"context": other},
            device_id_type=MESH,
        )

    for shift in range(1, nc):
        other, item = copy(shift)

        @pl.when(other < heads)
        def _():
            item.start()

    own = pltpu.make_async_copy(x_ref.at[jnp.minimum(me, heads - 1)], o_ref.at[me], loc)
    own.start()
    own.wait()

    @pl.when(me < heads)
    def _():
        for shift in range(1, nc):
            source = lax.rem(me + nc - shift, nc)
            pltpu.make_async_copy(o_ref.at[source], o_ref.at[source], recv.at[shift]).wait()

    for shift in range(1, nc):
        other, item = copy(shift)

        @pl.when(other < heads)
        def _():
            item.wait_send()


def to_heads(x, nc, collective_id):
    heads = x.shape[0]
    return pl.pallas_call(
        functools.partial(to_heads_kernel, nc, heads),
        out_shape=jax.ShapeDtypeStruct((nc,) + x.shape[1:], x.dtype),
        in_specs=[VM],
        out_specs=VM,
        scratch_shapes=[DMA((nc,)), DMA((nc,)), DMA],
        compiler_params=remote_params(collective_id),
    )(x)


def from_heads_kernel(nc, heads, x_ref, o_ref, send, recv, loc):
    me, _ = group_barrier(("context",), (nc,))

    def copy(shift):
        other = lax.rem(me + shift, nc)
        return pltpu.make_async_remote_copy(
            src_ref=x_ref.at[other],
            dst_ref=o_ref.at[jnp.minimum(me, heads - 1)],
            send_sem=send.at[shift],
            recv_sem=recv.at[shift],
            device_id={"context": other},
            device_id_type=MESH,
        )

    @pl.when(me < heads)
    def _():
        for shift in range(1, nc):
            copy(shift).start()
        own = pltpu.make_async_copy(x_ref.at[me], o_ref.at[me], loc)
        own.start()
        own.wait()

    for shift in range(1, nc):
        source = lax.rem(me + nc - shift, nc)

        @pl.when(source < heads)
        def _():
            at = jnp.minimum(source, heads - 1)
            pltpu.make_async_copy(o_ref.at[at], o_ref.at[at], recv.at[shift]).wait()

    @pl.when(me < heads)
    def _():
        for shift in range(1, nc):
            copy(shift).wait_send()


def from_heads(x, nc, heads, collective_id):
    return pl.pallas_call(
        functools.partial(from_heads_kernel, nc, heads),
        out_shape=jax.ShapeDtypeStruct((heads,) + x.shape[1:], x.dtype),
        in_specs=[VM],
        out_specs=VM,
        scratch_shapes=[DMA((nc,)), DMA((nc,)), DMA],
        compiler_params=remote_params(collective_id),
    )(x)


AXES = ("context", "tensor")


def rows_kernel(nc, nt, heads, x_ref, o_ref, send, recv, loc):
    me, total = group_barrier(AXES, (nc, nt))
    my_ctx, my_ten = lax.axis_index("context"), lax.axis_index("tensor")
    my_head = my_ten * heads + jnp.minimum(my_ctx, heads - 1)

    def copy(shift):
        other = lax.rem(me + shift, total)
        return pltpu.make_async_remote_copy(
            src_ref=x_ref.at[other],
            dst_ref=o_ref.at[my_head],
            send_sem=send.at[shift],
            recv_sem=recv.at[shift],
            device_id=spread(other, AXES, (nc, nt)),
            device_id_type=MESH,
        )

    @pl.when(my_ctx < heads)
    def _():
        for shift in range(1, total):
            copy(shift).start()
        own = pltpu.make_async_copy(x_ref.at[me], o_ref.at[my_head], loc)
        own.start()
        own.wait()

    for shift in range(1, total):
        source = lax.rem(me + total - shift, total)
        ctx, ten = lax.div(source, nt), lax.rem(source, nt)

        @pl.when(ctx < heads)
        def _():
            at = ten * heads + jnp.minimum(ctx, heads - 1)
            pltpu.make_async_copy(o_ref.at[at], o_ref.at[at], recv.at[shift]).wait()

    @pl.when(my_ctx < heads)
    def _():
        for shift in range(1, total):
            copy(shift).wait_send()


def to_rows(x, nc, nt, heads, collective_id):
    total = nc * nt
    return pl.pallas_call(
        functools.partial(rows_kernel, nc, nt, heads),
        out_shape=jax.ShapeDtypeStruct((nt * heads,) + x.shape[1:], x.dtype),
        in_specs=[VM],
        out_specs=VM,
        scratch_shapes=[DMA((total,)), DMA((total,)), DMA],
        compiler_params=remote_params(collective_id),
    )(x)


def rows_back_kernel(nc, nt, heads, x_ref, o_ref, send, recv, loc):
    me, total = group_barrier(AXES, (nc, nt))
    my_ctx, my_ten = lax.axis_index("context"), lax.axis_index("tensor")

    def copy(shift):
        other = lax.rem(me + shift, total)
        ctx, ten = lax.div(other, nt), lax.rem(other, nt)
        return ctx < heads, pltpu.make_async_remote_copy(
            src_ref=x_ref.at[ten * heads + jnp.minimum(ctx, heads - 1)],
            dst_ref=o_ref.at[me],
            send_sem=send.at[shift],
            recv_sem=recv.at[shift],
            device_id={"context": ctx, "tensor": ten},
            device_id_type=MESH,
        )

    for shift in range(1, total):
        goes, item = copy(shift)

        @pl.when(goes)
        def _():
            item.start()

    own = pltpu.make_async_copy(
        x_ref.at[my_ten * heads + jnp.minimum(my_ctx, heads - 1)], o_ref.at[me], loc
    )
    own.start()
    own.wait()

    @pl.when(my_ctx < heads)
    def _():
        for shift in range(1, total):
            source = lax.rem(me + total - shift, total)
            pltpu.make_async_copy(o_ref.at[source], o_ref.at[source], recv.at[shift]).wait()

    for shift in range(1, total):
        goes, item = copy(shift)

        @pl.when(goes)
        def _():
            item.wait_send()


def rows_back(x, nc, nt, heads, collective_id):
    total = nc * nt
    return pl.pallas_call(
        functools.partial(rows_back_kernel, nc, nt, heads),
        out_shape=jax.ShapeDtypeStruct((total,) + x.shape[1:], x.dtype),
        in_specs=[VM],
        out_specs=VM,
        scratch_shapes=[DMA((total,)), DMA((total,)), DMA],
        compiler_params=remote_params(collective_id),
    )(x)


def vectors_kernel(names, sizes, shared, x_ref, o_ref, now, *rest):
    bufs, sems = rest[: len(names)], rest[len(names) :]
    bar = pltpu.get_barrier_semaphore()
    for name, size in zip(names, sizes):
        me = lax.axis_index(name)
        for shift in range(1, size):
            pl.semaphore_signal(
                bar, inc=1, device_id={name: lax.rem(me + shift, size)}, device_id_type=MESH
            )
    pl.semaphore_wait(bar, sum(sizes) - len(sizes))
    for stage, (name, size) in enumerate(zip(names, sizes)):
        buf, send, recv = bufs[stage], sems[2 * stage], sems[2 * stage + 1]
        me = lax.axis_index(name)

        def copy(shift):
            return pltpu.make_async_remote_copy(
                src_ref=now.at[stage] if stage else x_ref.at[0],
                dst_ref=buf.at[me],
                send_sem=send.at[shift],
                recv_sem=recv.at[shift],
                device_id={name: lax.rem(me + shift, size)},
                device_id_type=MESH,
            )

        for shift in range(1, size):
            copy(shift).start()
        buf[me] = now[stage] if stage else x_ref[0]
        for shift in range(1, size):
            source = lax.rem(me + size - shift, size)
            pltpu.make_async_copy(buf.at[source], buf.at[source], recv.at[shift]).wait()
        total = buf[0]
        for at in range(1, size):
            total = total + buf[at]
        if stage == 0:
            row = lax.broadcasted_iota(jnp.int32, total.shape, 0)
            total = jnp.where(row < shared, total, x_ref[0])
        if stage + 1 < len(names):
            now[stage + 1] = total
        else:
            o_ref[...] = total
        for shift in range(1, size):
            copy(shift).wait_send()


def sum_vectors(rows, shared, mesh_sizes, collective_id):
    names = ("tensor", "context", "dp")
    sizes = tuple(mesh_sizes[name] for name in names)
    shape = rows.shape
    return pl.pallas_call(
        functools.partial(vectors_kernel, names, sizes, shared),
        out_shape=jax.ShapeDtypeStruct(shape, jnp.float32),
        in_specs=[VM],
        out_specs=VM,
        scratch_shapes=[pltpu.VMEM((len(names),) + shape, jnp.float32)]
        + [pltpu.VMEM((size,) + shape, jnp.float32) for size in sizes]
        + [DMA((size,)) for size in sizes for _ in range(2)],
        compiler_params=remote_params(collective_id),
    )(rows[None])


def dot(left, right, dims):
    return lax.dot_general(left, right, ((dims[0], dims[1]), ((), ())), preferred_element_type=jnp.float32)


def key_positions(first, keys, queries):
    return first + lax.broadcasted_iota(jnp.int32, (keys, queries), 0)


def load_rows(qkv_ref, rows, nb, half, qs, kt, ks, vs):
    for block in range(nb):
        part = slice(block % 2 * half, block % 2 * half + half)
        item = qkv_ref[block // 2, :, part]
        qs[block] = item[:HEAD_DIM] * jnp.asarray(HEAD_DIM**-0.5, item.dtype)
        if kt is not None:
            kt[block] = item[HEAD_DIM : 2 * HEAD_DIM]
        ks[block] = item[HEAD_DIM : 2 * HEAD_DIM].T
        if vs is not None:
            vs[block] = item[2 * HEAD_DIM :].T


def forward_kernel(half, slot_ref, low_ref, on_ref, qkv_ref, start_ref, o_ref, full_ref, lse_ref, qs, ks):
    nb = full_ref.shape[0]

    @pl.when(on_ref[0] > 0)
    def _():
        load_rows(qkv_ref, None, nb, half, qs, None, ks, None)

        @pl.loop(0, nb)
        def _(nq):
            slot = slot_ref[nq]
            query = qs[slot]
            start = start_ref[nq]
            here = nq * half + lax.broadcasted_iota(jnp.int32, (1, half), 1)

            def step(nk, state):
                top, total, acc = state
                at = slot_ref[nk]
                score = dot(ks[at], query, ((1,), (0,)))
                place = key_positions(nk * half, half, half)
                score = jnp.where((place >= start) & (place <= here), score, NEG_FILL)
                new_top = jnp.maximum(top, jnp.max(score, axis=0, keepdims=True))
                factor = jnp.exp(top - new_top)
                weight = jnp.exp(score - new_top)
                total = total * factor + jnp.sum(weight, axis=0, keepdims=True)
                value = qkv_ref[at // 2, 2 * HEAD_DIM :, pl.ds(pl.multiple_of(at % 2 * half, 128), half)]
                acc = acc * factor + dot(value, weight.astype(jnp.bfloat16), ((1,), (0,)))
                return new_top, total, acc

            top, total, acc = lax.fori_loop(
                low_ref[nq],
                nq + 1,
                step,
                (
                    jnp.full((1, half), NEG_FILL, jnp.float32),
                    jnp.zeros((1, half), jnp.float32),
                    jnp.zeros((HEAD_DIM, half), jnp.float32),
                ),
            )
            result = acc / total
            full_ref[slot] = result
            lse_ref[slot] = top + jnp.log(total)
            low = result.astype(jnp.bfloat16)
            o_ref[2 * slot] = low[:, : half // 2]
            o_ref[2 * slot + 1] = low[:, half // 2 :]


def attend_forward(qkv, tables, half):
    nc = qkv.shape[0]
    nb = 2 * nc
    return pl.pallas_call(
        functools.partial(forward_kernel, half),
        out_shape=(
            jax.ShapeDtypeStruct((2 * nb, HEAD_DIM, half // 2), jnp.bfloat16),
            jax.ShapeDtypeStruct((nb, HEAD_DIM, half), jnp.float32),
            jax.ShapeDtypeStruct((nb, 1, half), jnp.float32),
        ),
        in_specs=[SM, SM, SM, VM, VM],
        out_specs=(VM, VM, VM),
        scratch_shapes=[
            pltpu.VMEM((nb, HEAD_DIM, half), jnp.bfloat16),
            pltpu.VMEM((nb, half, HEAD_DIM), jnp.bfloat16),
        ],
        compiler_params=pltpu.CompilerParams(vmem_limit_bytes=48 << 20),
    )(tables["slot"], tables["low"], tables["on"], qkv, tables["start"])


def backward_kernel(
    half, slot_ref, high_ref, on_ref, qkv_ref, start_ref, full_ref, lse_ref, grad_ref, o_ref, qs, kt, ks, vs, gs, ds, dq
):
    nb = full_ref.shape[0]

    @pl.when(on_ref[0] > 0)
    def _():
        load_rows(qkv_ref, None, nb, half, qs, kt, ks, vs)
        for block in range(nb):
            both = jnp.concatenate([grad_ref[2 * block], grad_ref[2 * block + 1]], axis=1)
            gs[block] = both
            ds[block] = jnp.sum(both.astype(jnp.float32) * full_ref[block], axis=0, keepdims=True)
            dq[block] = jnp.zeros((HEAD_DIM, half), jnp.float32)

        @pl.loop(0, nb)
        def _(nk):
            at = slot_ref[nk]
            place = key_positions(nk * half, half, half)

            def step(nq, state):
                grad_key, grad_value = state
                slot = slot_ref[nq]
                query, grad = qs[slot], gs[slot]
                here = nq * half + lax.broadcasted_iota(jnp.int32, (1, half), 1)
                score = dot(ks[at], query, ((1,), (0,)))
                score = jnp.where((place >= start_ref[nq]) & (place <= here), score, NEG_FILL)
                weight = jnp.exp(score - lse_ref[slot])
                grad_weight = dot(vs[at], grad, ((1,), (0,)))
                grad_score = (weight * (grad_weight - ds[slot])).astype(jnp.bfloat16)
                grad_value = grad_value + dot(grad, weight.astype(jnp.bfloat16), ((1,), (1,)))
                grad_key = grad_key + dot(query, grad_score, ((1,), (1,)))
                dq[slot] += dot(kt[at], grad_score, ((1,), (0,)))
                return grad_key, grad_value

            zero = jnp.zeros((HEAD_DIM, half), jnp.float32)
            grad_key, grad_value = lax.fori_loop(nk, high_ref[nk], step, (zero, zero))
            columns = pl.ds(pl.multiple_of(at % 2 * half, 128), half)
            o_ref[at // 2, HEAD_DIM : 2 * HEAD_DIM, columns] = grad_key.astype(jnp.bfloat16)
            o_ref[at // 2, 2 * HEAD_DIM :, columns] = grad_value.astype(jnp.bfloat16)

        for block in range(nb):
            part = slice(block % 2 * half, block % 2 * half + half)
            o_ref[block // 2, :HEAD_DIM, part] = (dq[block] * HEAD_DIM**-0.5).astype(jnp.bfloat16)


def attend_backward(qkv, tables, full, lse, grad, half):
    nc = qkv.shape[0]
    nb = 2 * nc
    low = jnp.bfloat16
    return pl.pallas_call(
        functools.partial(backward_kernel, half),
        out_shape=jax.ShapeDtypeStruct(qkv.shape, low),
        in_specs=[SM, SM, SM, VM, VM, VM, VM, VM],
        out_specs=VM,
        scratch_shapes=[
            pltpu.VMEM((nb, HEAD_DIM, half), low),
            pltpu.VMEM((nb, HEAD_DIM, half), low),
            pltpu.VMEM((nb, half, HEAD_DIM), low),
            pltpu.VMEM((nb, half, HEAD_DIM), low),
            pltpu.VMEM((nb, HEAD_DIM, half), low),
            pltpu.VMEM((nb, 1, half), jnp.float32),
            pltpu.VMEM((nb, HEAD_DIM, half), jnp.float32),
        ],
        compiler_params=pltpu.CompilerParams(vmem_limit_bytes=48 << 20),
    )(tables["slot"], tables["high"], tables["on"], qkv, tables["start"], full, lse, grad)


def block_tables(segments, order, half, heads):
    nb = order.shape[0]
    counts = jnp.arange(nb, dtype=jnp.int32)
    slot = jnp.sum(jnp.where(order[None, :] == counts[:, None], counts[None, :], 0), axis=1)
    docs = jnp.arange(DOC_LIMIT, dtype=jnp.int32)
    before = jnp.sum((segments[None, :] < docs[:, None]).astype(jnp.int32), axis=1)
    start = jnp.sum(jnp.where(segments[None, :] == docs[:, None], before[:, None], 0), axis=0)
    blocks = segments.reshape(nb, half)
    first, last = blocks[:, 0], blocks[:, -1]
    low = jnp.sum((last[None, :] < first[:, None]).astype(jnp.int32), axis=1)
    high = jnp.sum((first[None, :] <= last[:, None]).astype(jnp.int32), axis=1)
    on = (lax.axis_index("context") < heads).astype(jnp.int32).reshape(1)
    return {"slot": slot, "low": low, "high": high, "on": on, "start": start.reshape(nb, 1, half)}


def norm_parts(values):
    centre = jnp.mean(values, axis=-1, keepdims=True)
    shifted = values - centre
    spread_ = jnp.mean(shifted * shifted, axis=-1, keepdims=True)
    scale = lax.rsqrt(spread_ + NORM_EPS)
    return shifted * scale, scale


def norm_backward(grad, normed, scale, gain):
    e = grad * gain
    mean_e = jnp.mean(e, axis=-1, keepdims=True)
    mean_en = jnp.mean(e * normed, axis=-1, keepdims=True)
    return (e - mean_e - normed * mean_en) * scale


def gelu_tanh(values):
    return jax.nn.gelu(values, approximate=True)


def cross_rows(left, right):
    return lax.dot_general(
        left, right, (((0,), (0,)), ((), ())), preferred_element_type=jnp.float32
    )


def after(value, done):
    return lax.optimization_barrier((value, done))[0]


def per_device(
    mesh_sizes,
    inputs,
    first_gain,
    first_shift,
    project_weight,
    project_bias,
    attend_weight,
    attend_bias,
    second_gain,
    second_shift,
    expand_weight,
    expand_bias,
    shrink_weight,
    shrink_bias,
    segments,
    block_order,
    cotangent,
):
    nt, nc = mesh_sizes["tensor"], mesh_sizes["context"]
    own_rows, width = inputs.shape[1], inputs.shape[2]
    local_width = project_weight.shape[2]
    heads = local_width // HEAD_DIM
    block_rows = own_rows * nt
    half = block_rows // 2
    low = jnp.bfloat16
    tables = block_tables(segments[0], block_order, half, heads)

    tokens_own = inputs[0].astype(jnp.float32)
    grad_out = cotangent[0]
    normed1, scale1 = norm_parts(tokens_own)
    hidden1 = (normed1 * first_gain + first_shift).astype(low)
    hidden1_full = gather_rows(hidden1, nt, 0)

    attend_full = lax.all_gather(after(attend_weight, hidden1_full), "tensor", axis=0, tiled=True)
    grad_full = lax.all_gather(after(grad_out, attend_full), "tensor", axis=0, tiled=True)

    by_head = project_weight.reshape(3, width, heads, HEAD_DIM)
    bias = jnp.stack([project_bias[0], jnp.zeros_like(project_bias[0]), project_bias[1]])
    bias = bias.reshape(3, heads, HEAD_DIM).transpose(1, 0, 2).reshape(-1, 1)
    weight_rows = by_head.transpose(2, 0, 3, 1).reshape(3 * local_width, width)
    projected = dot(weight_rows, hidden1_full, ((1,), (1,))) + bias
    qkv = to_heads(projected.astype(low).reshape(heads, 3 * HEAD_DIM, block_rows), nc, 1)
    pieces, attended_full, lse = attend_forward(qkv, tables, half)
    attended = to_rows(pieces, nc, nt, heads, 2).reshape(width, own_rows)

    middle = tokens_own + cross_rows(attended, attend_full) + attend_bias
    normed2, scale2 = norm_parts(middle)
    hidden2 = (normed2 * second_gain + second_shift).astype(low)
    hidden2_full = gather_rows(hidden2, nt, 3)
    pre_act = jnp.dot(hidden2_full, expand_weight, preferred_element_type=jnp.float32) + expand_bias
    activ = gelu_tanh(pre_act).astype(low)
    grad_act = dot(grad_full, shrink_weight, ((1,), (1,)))
    grad_pre = jax.vjp(gelu_tanh, pre_act)[1](grad_act)[0].astype(low)
    grad_hidden2 = scatter_rows(dot(grad_pre, expand_weight, ((1,), (1,))).astype(low), nt, 4)

    feed = jnp.dot(activ, shrink_weight, preferred_element_type=jnp.float32).astype(low)
    feed_sum = lax.psum_scatter(
        after(feed, grad_hidden2), "tensor", scatter_dimension=0, tiled=True
    ).astype(jnp.float32)
    outputs = (middle + feed_sum + shrink_bias).astype(low)[None]

    grad_shrink = cross_rows(activ, grad_full).astype(low)
    grad_expand = cross_rows(hidden2_full, grad_pre).astype(low)
    grad_expand_bias = jnp.sum(grad_pre.astype(jnp.float32), axis=0)
    grad_shrink_bias = jnp.sum(grad_out.astype(jnp.float32), axis=0)
    grad_shrink, grad_expand = lax.psum((grad_shrink, grad_expand), ("context", "dp"))

    grad_second_gain = jnp.sum(grad_hidden2 * normed2, axis=0)
    grad_second_shift = jnp.sum(grad_hidden2, axis=0)
    grad_middle = grad_out.astype(jnp.float32) + norm_backward(
        grad_hidden2, normed2, scale2, second_gain
    )
    grad_middle_low = grad_middle.astype(low)
    grad_attend_bias = jnp.sum(grad_middle_low.astype(jnp.float32), axis=0)
    grad_attended = dot(attend_full, grad_middle_low, ((1,), (1,))).astype(low)
    grad_heads = rows_back(
        grad_attended.reshape(nt * heads, HEAD_DIM, own_rows), nc, nt, heads, 5
    )
    grad_attend = jnp.dot(attended, grad_middle_low, preferred_element_type=jnp.float32).astype(low)
    grad_attend = lax.psum_scatter(grad_attend, "tensor", scatter_dimension=0, tiled=True)
    grad_attend = lax.psum(grad_attend, ("context", "dp"))

    grad_qkv = attend_backward(qkv, tables, attended_full, lse, grad_heads, half)
    grad_rows = from_heads(grad_qkv, nc, heads, 6).reshape(3 * local_width, block_rows)
    grad_hidden1 = scatter_rows(cross_rows(grad_rows, weight_rows).astype(low), nt, 7)
    grad_project = dot(hidden1_full, grad_rows, ((0,), (1,))).astype(low)
    grad_project = lax.psum(grad_project, ("context", "dp"))
    grad_project = (
        grad_project.reshape(width, heads, 3, HEAD_DIM).transpose(2, 0, 1, 3).reshape(3, width, local_width)
    )
    row_sums = jnp.sum(grad_rows.astype(jnp.float32), axis=1).reshape(heads, 3, HEAD_DIM)
    grad_project_bias = jnp.concatenate([row_sums[:, 0].reshape(-1), row_sums[:, 2].reshape(-1)])

    grad_first_gain = jnp.sum(grad_hidden1 * normed1, axis=0)
    grad_first_shift = jnp.sum(grad_hidden1, axis=0)
    grad_inputs = (grad_middle + norm_backward(grad_hidden1, normed1, scale1, first_gain)).astype(low)[None]

    spare = -grad_project_bias.shape[0] % width
    vectors = jnp.concatenate(
        [
            grad_first_gain,
            grad_first_shift,
            grad_attend_bias,
            grad_second_gain,
            grad_second_shift,
            grad_shrink_bias,
            grad_expand_bias,
            jnp.pad(grad_project_bias, (0, spare)),
        ]
    ).reshape(-1, width)
    summed = sum_vectors(vectors, 6, mesh_sizes, 8)
    tail = summed[6:].reshape(-1)
    wide = grad_expand_bias.shape[0]
    f32 = lambda value: value.astype(jnp.float32)
    return (
        outputs,
        grad_inputs,
        summed[0],
        summed[1],
        f32(grad_project),
        tail[wide : wide + 2 * local_width].reshape(2, local_width),
        f32(grad_attend),
        summed[2],
        summed[3],
        summed[4],
        f32(grad_expand),
        tail[:wide],
        f32(grad_shrink),
        summed[5],
    )


def solution(mesh):
    rows = P("dp", ("context", "tensor"), None)
    in_specs = (
        rows,
        P(),
        P(),
        P(None, None, "tensor"),
        P(None, "tensor"),
        P("tensor", None),
        P(),
        P(),
        P(),
        P(None, "tensor"),
        P("tensor"),
        P("tensor", None),
        P(),
        P("dp", None),
        P(),
        rows,
    )
    out_specs = (
        rows,
        rows,
        P(),
        P(),
        P(None, None, "tensor"),
        P(None, "tensor"),
        P("tensor", None),
        P(),
        P(),
        P(),
        P(None, "tensor"),
        P("tensor"),
        P("tensor", None),
        P(),
    )
    return jax.shard_map(
        functools.partial(per_device, dict(mesh.shape)),
        mesh=mesh,
        in_specs=in_specs,
        out_specs=out_specs,
        check_vma=False,
    )
```

time: 609 us -> 388 us (0.64)
  Pallas kernels: 0 us -> 231 us
  waiting for transfers between devices: 312 us -> 88.7 us
  local copies, waits for them, and re-layouts: 76.5 us -> 10.8 us
  matrix products: 80 us -> 23.7 us
  blocking collectives: 54.9 us -> 0 us
  other arithmetic: 50.8 us -> 19.7 us
  loops' own time: 16 us -> 0 us
    pallas_call x0 -> x11, Pallas kernels: none -> 231 us  [the longest x2 65.3 us: gather_rows(): pl.pallas_call(functools.partial(gather_kernel, n), out_shape=jax.ShapeDt...]
    all_gather x6 -> x2, waiting for transfers between devices: 123 us -> 0.02 us  [the longest x1 0.02 us: per_device(): lax.all_gather(after(attend_weight, hidden1_full), 'tensor', axis=0, tile...]
    reduce_scatter x5 -> x2, waiting for transfers between devices: 117 us -> 31.3 us  [the longest x1 31.3 us: per_device(): lax.psum_scatter(after(feed, grad_hidden2), 'tensor', scatter_dimension=0...]
    psum x2 -> x0, blocking collectives: 54.9 us -> none  [the longest x1 40.2 us: per_device(): lax.psum((grad_first_gain, grad_first_shift, grad_attend_bias, grad_secon...]
    dot_general x35 -> x7, matrix products: 65.1 us -> 13.3 us  [the longest x5 9.16 us: dot(): lax.dot_general(left, right, ((dims[0], dims[1]), ((), ())), preferred_el...]
    dynamic_slice x34 -> x0, local copies, waits for them, and re-layouts: 33.4 us -> none  [the longest x12 13.6 us: over_blocks(): running, _ = lax.scan(inner, running, (stacked, starts))]
    gather x1 -> x0, local copies, waits for them, and re-layouts: 17.4 us -> none  [per_device(): seg_stored = jnp.take(segments[0], places)]
    another operation x2 -> x0, loops' own time: 16 us -> none  [the longest x1 8.04 us: per_device(): grad_query, key_terms = lax.scan(key_pass, zero_rows, key_starts)]
  transfers between devices with their start and end apart: 12 -> 5, of which waited for: 11 -> 2; matrix products, arithmetic and copies ran while one was open for 9% -> 7% of each run, Pallas kernels for 0% -> 46%
where the time goes in v1:
time: 388 us; the launch traced here: 389 us
  Pallas kernels  231 us (60%)
  waiting for transfers between devices  88.7 us (23%)
  matrix products  23.7 us (6%)
  other arithmetic  19.7 us (5%)
  between operations  14.6 us (4%)
  local copies, waits for them, and re-layouts  10.8 us (3%)
    pallas_call x2, Pallas kernels, gather_rows(): pl.pallas_call(functools.partial(gather_kernel, n), out_shape=jax.ShapeDt...  65.3 us
    pallas_call x2, Pallas kernels, scatter_rows(): pl.pallas_call(functools.partial(scatter_kernel, n), out_shape=jax.ShapeD...  58.9 us
    psum x1, waiting for transfers between devices, per_device(): grad_project = lax.psum(grad_project, ('context', 'dp'))  57.3 us
    reduce_scatter x1, waiting for transfers between devices, per_device(): lax.psum_scatter(after(feed, grad_hidden2), 'tensor', scatter_dimension=0...  31.3 us
    pallas_call x1, Pallas kernels, rows_back(): pl.pallas_call(functools.partial(rows_back_kernel, nc, nt, heads), out_sh...  22 us
    pallas_call x1, Pallas kernels, to_rows(): pl.pallas_call(functools.partial(rows_kernel, nc, nt, heads), out_shape=j...  20.7 us
    pallas_call x1, Pallas kernels, attend_backward(): pl.pallas_call(functools.partial(backward_kernel, half), out_shape=jax.Sh...  15.2 us
    pallas_call x1, Pallas kernels, from_heads(): pl.pallas_call(functools.partial(from_heads_kernel, nc, heads), out_shape...  13.8 us
  transfers between devices with their start and end apart: 5, of which 2 were waited for; matrix products, arithmetic and copies ran while one was open for 7% of the time, Pallas kernels for 46%

profile of v1, /device:TPU:0, one launch (start us, length us, event | category | flops | bytes accessed | tf_op | source)
XLA Modules:
  0.0 388.6 jit_solution(6001772048182025232)
XLA Ops:
  7.3 1.2 convert_reduce_fusion.3
  8.5 1.2 fusion.23
  9.7 1.2 fusion.16.x_ref
  10.9 25.6 %shard_map.263 = bf16[4,192,768]{2,1,0:T(8,128)(2,1)S(1)} custom-call(bf16[192,768]{1,0:T(8,128)(2,1)S(1)} %fusion.16.x_ref), custom_call_target="tpu_custom_call" | custom-call | tf_op jit(solution)/shard_map/pallas_call | solution.py:96
  36.8 0.1 reshape.144
  37.0 0.5 broadcast.141
  37.5 0.7 reduce.23
  38.3 0.1 copy.51
  38.4 0.1 copy.52
  38.5 0.9 add_convert_fusion
  39.5 10.0 %shard_map.264.qkv_ref = bf16[4,192,768]{2,1,0:T(8,128)(2,1)S(1)} custom-call(bf16[3,192,768]{2,1,0:T(8,128)(2,1)S(1)} %bitcast.104), custom_call_target="tpu_custom_call" | custom-call | tf_op jit(solution)/shard_map/pallas_call | solution.py:254
  49.5 0.1 convert_reduce_fusion.5
  49.7 0.7 convert_reduce_fusion.6
  50.4 0.1 select_reduce_fusion
  50.5 12.3 %shard_map.265 = (bf16[16,64,192]{2,1,0:T(8,128)(2,1)S(1)}, f32[8,64,384]{2,1,0:T(8,128)S(1)}, f32[8,1,384]{2,1,0:T(1,128)S(1)}) custom-call(s32[8]{0:T(128)S(1)} %get-tuple-element.61.slot_ref, s32[8]{0:T(128)S(1)} %get-tuple-element.44.low_ref, s32[1]{0:T(128)} %bitcast.3.on_ref, bf16[4,192,768]{2,1,0:T(8,128)(2,1)S(1)} %shard_map.264.qkv_ref, ...), custom_call_target="tpu_custom_call" | custom-call | tf_op jit(solution)/shard_map/pallas_call | solution.py:549
  62.8 0.9 copy-done.4
  63.7 0.6 copy-done.6
  64.3 20.7 %shard_map.266 = bf16[12,64,192]{2,1,0:T(8,128)(2,1)S(1)} custom-call(bf16[16,64,192]{2,1,0:T(8,128)(2,1)S(1)} %get-tuple-element.20.x_ref), custom_call_target="tpu_custom_call" | custom-call | tf_op jit(solution)/shard_map/pallas_call | solution.py:355
  85.1 1.8 fusion.32
  87.0 0.2 multiply_reduce_fusion.2
  87.2 0.2 add_convert_fusion.2.x_ref
  87.4 39.6 %shard_map.267 = bf16[4,192,768]{2,1,0:T(8,128)(2,1)S(1)} custom-call(bf16[192,768]{1,0:T(8,128)(2,1)S(1)} %add_convert_fusion.2.x_ref), custom_call_target="tpu_custom_call" | custom-call | tf_op jit(solution)/shard_map/pallas_call | solution.py:96
  127.1 1.1 fusion.33
  128.2 1.4 copy-done.43
  129.6 2.6 convolution_convert_fusion.5
  132.2 5.0 %convert_reduce_fusion = (f32[768]{0:T(1024)}, bf16[768,768]{1,0:T(8,128)(2,1)S(1)}) fusion(f32[768,768]{1,0:T(8,128)} %copy-done.43, f32[768]{0:T(1024)S(1)} %copy-done.42, bf16[768,768]{1,0:T(8,128)(2,1)} %all-gather.5.cloned.1.call-done, bf16[768,768]{1,0:T(8,128)(2,1)S(1)} %copy-done), kind=kOutput, calls=%fused_computation.9 | convolution fusion | flops 919534848 | bytes 5904384 | tf_op jit(solution)/shard_map/dot_general | solution.py:481
  137.3 1.1 convolution_convert_fusion.4
  138.4 26.6 %shard_map.268 = f32[192,768]{1,0:T(8,128)S(1)} custom-call(bf16[4,192,768]{2,1,0:T(8,128)(2,1)S(1)} %bitcast.103), custom_call_target="tpu_custom_call" | custom-call | tf_op jit(solution)/shard_map/pallas_call | solution.py:169
  165.1 2.0 multiply_reduce_fusion
  167.1 31.3 %reduce-scatter.3.cloned.1.call-done = bf16[192,768]{1,0:T(8,128)(2,1)} async-done(((bf16[768,768]{1,0:T(8,128)(2,1)}), bf16[192,768]{1,0:T(8,128)(2,1)}) %reduce-scatter.3.cloned.1.call-update) | async-done | bytes 294928 | tf_op jit(solution)/shard_map/reduce_scatter | solution.py:734
  198.4 2.8 convert_reduce_fusion.4
  201.2 0.8 copy-done.12
  202.0 1.5 convolution_convert_fusion.2
  203.5 0.2 all-reduce.4.cloned.1.call-start
  203.8 3.9 %convolution_convert_fusion.1 = bf16[768,768]{1,0:T(8,128)(2,1)} fusion(bf16[768,768]{1,0:T(8,128)(2,1)} %bitcast.101, bf16[768,768]{1,0:T(8,128)(2,1)} %copy-done.45), kind=kOutput, calls=%fused_computation.14 | convolution fusion | flops 906559488 | bytes 3538944 | tf_op jit(solution)/shard_map/dot_general | solution.py:668
  207.8 2.5 convolution_convert_fusion
  210.2 1.3 convolution_convert_fusion.7
  211.5 1.1 copy.49
  212.6 22.0 %shard_map.269.grad_ref = bf16[16,64,192]{2,1,0:T(8,128)(2,1)S(1)} custom-call(bf16[12,64,192]{2,1,0:T(8,128)(2,1)S(1)} %bitcast.97), custom_call_target="tpu_custom_call" | custom-call | tf_op jit(solution)/shard_map/pallas_call | solution.py:410
  234.7 0.7 copy-done.7
  235.4 0.7 copy-done.8
  236.0 15.2 %shard_map.270.x_ref = bf16[4,192,768]{2,1,0:T(8,128)(2,1)S(1)} custom-call(s32[8]{0:T(128)S(1)} %get-tuple-element.61.slot_ref, s32[8]{0:T(128)S(1)} %copy-done.8, s32[1]{0:T(128)} %bitcast.3.on_ref, bf16[4,192,768]{2,1,0:T(8,128)(2,1)S(1)} %shard_map.264.qkv_ref, s32[8,1,384]{2,1,0:T(1,128)S(1)} %bitcast.106, f32[8,64,384]{2,1,0:T(8,128)S(1)} %copy-done.5, ...), custom_call_target="tpu_custom_call" | custom-call | tf_op jit(solution)/shard_map/pallas_call | solution.py:615
  251.2 13.8 %shard_map.271 = bf16[3,192,768]{2,1,0:T(8,128)(2,1)S(1)} custom-call(bf16[4,192,768]{2,1,0:T(8,128)(2,1)S(1)} %shard_map.270.x_ref), custom_call_target="tpu_custom_call" | custom-call | tf_op jit(solution)/shard_map/pallas_call | solution.py:301
  265.1 0.9 convolution_convert_fusion.6
  265.9 1.0 copy.50
  266.9 0.2 convert_reduce_fusion.1
  267.1 0.1 reshape.153
  267.2 0.2 copy-done.20
  267.4 1.1 convolution_convert_fusion.3
  268.6 32.3 %shard_map.272 = f32[192,768]{1,0:T(8,128)S(1)} custom-call(bf16[4,192,768]{2,1,0:T(8,128)(2,1)S(1)} %bitcast.102), custom_call_target="tpu_custom_call" | custom-call | tf_op jit(solution)/shard_map/pallas_call | solution.py:169
  300.9 0.4 fusion.22
  301.4 0.1 reshape_squeeze.10
  301.5 0.1 reshape_squeeze.11
  301.6 0.4 copy-done.26
  302.3 12.5 %shard_map.273 = f32[8,768]{1,0:T(8,128)S(1)} custom-call(f32[1,8,768]{2,1,0:T(8,128)S(1)} %broadcast_in_dim_reshape.3.x_ref), custom_call_target="tpu_custom_call" | custom-call | tf_op jit(solution)/shard_map/pallas_call | solution.py:468
  314.9 0.6 slice.73
  315.5 0.7 slice_reduce_fusion
  316.1 1.0 fusion.25
  317.1 57.3 %all-reduce.4.cloned.1.call-done = (bf16[3,768,192]{1,2,0:T(8,128)(2,1)}, bf16[192,768]{1,0:T(8,128)(2,1)}, bf16[768,768]{1,0:T(8,128)(2,1)}, bf16[768,768]{1,0:T(8,128)(2,1)}) async-done(((bf16[3,768,192]{1,2,0:T(8,128)(2,1)}, bf16[192,768]{1,0:T(8,128)(2,1)}, bf16[768,768]{1,0:T(8,128)(2,1)}, bf16[768,768]{1,0:T(8,128)(2,1)}), (bf16[3,768,192]{1,2,0:T(8,128)(2,1)}, bf16[192,768]{1,0:T(8,128)(2,1)}, ...) | async-done | bytes 3538960 | tf_op jit(solution)/shard_map/psum | solution.py:764
  374.4 1.9 convert_element_type.136
  376.3 2.5 convert_element_type.134
  378.8 1.6 convert_element_type.138
  380.4 0.1 copy-done.16
  380.5 1.6 convert_element_type.140
  (124 shorter events, 1.2 us)
Async XLA Ops:
  7.2 122.4 %copy-start = (bf16[768,768]{1,0:T(8,128)(2,1)S(1)}, bf16[768,768]{1,0:T(8,128)(2,1)}, u32[]{:S(2)}) copy-start(bf16[768,768]{1,0:T(8,128)(2,1)} %param.27) | copy-start | bytes 3538948
  7.2 29.6 %copy-start.37 = (f32[2,192]{1,0:T(2,128)S(1)}, f32[2,192]{1,0:T(2,128)}, u32[]{:S(2)}) copy-start(f32[2,192]{1,0:T(2,128)} %param.20) | copy-start | bytes 4612
  7.2 30.3 %copy-start.21 = (s32[1,3072]{1,0:T(1,128)S(1)}, s32[1,3072]{1,0:T(1,128)}, u32[]{:S(2)}) copy-start(s32[1,3072]{1,0:T(1,128)} %param.29) | copy-start | bytes 36868
  7.2 31.2 %copy-start.18 = (bf16[3,768,192]{1,2,0:T(8,128)(2,1)S(1)}, bf16[3,768,192]{1,2,0:T(8,128)(2,1)}, u32[]{:S(2)}) copy-start(bf16[3,768,192]{1,2,0:T(8,128)(2,1)} %param.19) | copy-start | bytes 2654212
  7.2 77.8 %all-gather.3.cloned.1.call-start = ((), (), s32[]{:S(2)}) async-start(), calls=%async_computation.2 | async-start | bytes 1474560 | tf_op jit(solution)/shard_map/all_gather | solution.py:711
  8.5 28.1 %copy-start.24 = (f32[192]{0:T(256)}, f32[192]{0:T(256)S(1)}, u32[]{:S(2)}) copy-start(f32[192]{0:T(256)S(1)} %broadcast_multiply_fusion.5) | copy-start | bytes 2308
  9.7 26.9 %copy-start.27 = (f32[192]{0:T(256)}, f32[192]{0:T(256)S(1)}, u32[]{:S(2)}) copy-start(f32[192]{0:T(256)S(1)} %add_rsqrt_fusion.1) | copy-start | bytes 2308
  36.6 2.9 copy-start.1
  36.6 95.6 %all-gather.5.cloned.1.call-start = ((), (), s32[]{:S(2)}) async-start(), calls=%async_computation.3 | async-start | bytes 1474560 | tf_op jit(solution)/shard_map/all_gather | solution.py:712
  38.5 0.9 copy-start.19
  39.5 10.2 %copy-start.38 = (s32[8]{0:T(128)S(1)}, s32[8]{0:T(128)}, u32[]{:S(2)}) copy-start(s32[8]{0:T(128)} %param.30) | copy-start | bytes 100
  39.5 45.6 %copy-start.10 = (bf16[1,192,768]{2,1,0:T(8,128)(2,1)S(1)}, bf16[1,192,768]{2,1,0:T(8,128)(2,1)}, u32[]{:S(2)}) copy-start(bf16[1,192,768]{2,1,0:T(8,128)(2,1)} %param.16) | copy-start | bytes 884740
  39.5 45.6 %copy-start.33 = (f32[768]{0:T(1024)S(1)}, f32[768]{0:T(1024)}, u32[]{:S(2)}) copy-start(f32[768]{0:T(1024)} %param.22) | copy-start | bytes 9220
  62.8 0.9 copy-start.4
  63.7 0.6 copy-start.6
  85.0 2.2 copy-start.22
  85.0 2.2 copy-start.34
  85.1 113.3 %reduce-scatter.3.cloned.1.call-start = ((), (), s32[]{:S(2)}) async-start(), calls=%async_computation.4 | async-start | bytes 1474560 | tf_op jit(solution)/shard_map/reduce_scatter | solution.py:734
  86.9 41.2 %copy-start.9 = (f32[192,768]{1,0:T(8,128)}, f32[192,768]{1,0:T(8,128)S(1)}, u32[]{:S(2)}) copy-start(f32[192,768]{1,0:T(8,128)S(1)} %get-tuple-element.60) | copy-start | bytes 1769476
  87.0 40.1 %copy-start.39 = (bf16[768,768]{1,0:T(8,128)(2,1)S(1)}, bf16[768,768]{1,0:T(8,128)(2,1)}, u32[]{:S(2)}) copy-start(bf16[768,768]{1,0:T(8,128)(2,1)} %param.25) | copy-start | bytes 3538948
  127.0 1.1 copy-start.3
  127.1 2.5 copy-start.42
  128.2 1.4 copy-start.43
  132.2 5.0 %copy-start.40 = (bf16[768,768]{1,0:T(8,128)(2,1)S(1)}, bf16[768,768]{1,0:T(8,128)(2,1)}, u32[]{:S(2)}) copy-start(bf16[768,768]{1,0:T(8,128)(2,1)} %param.25) | copy-start | bytes 3538948
  137.3 1.1 copy-start.45
  138.4 60.0 %copy-start.35 = (f32[768]{0:T(1024)S(1)}, f32[768]{0:T(1024)}, u32[]{:S(2)}) copy-start(f32[768]{0:T(1024)} %param.28) | copy-start | bytes 9220
  165.0 136.3 %reduce-scatter.5.cloned.1.call-start = ((), (), s32[]{:S(2)}) async-start(), calls=%async_computation.5 | async-start | bytes 1474560 | tf_op jit(solution)/shard_map/reduce_scatter | solution.py:757
  201.2 0.8 copy-start.12
  203.5 170.8 %all-reduce.4.cloned.1.call-start = ((), (), s32[]{:S(2)}) async-start(), calls=%async_computation.6 | async-start | bytes 7077888 | tf_op jit(solution)/shard_map/psum | solution.py:764
  203.8 4.0 %copy-start.41 = (bf16[768,768]{1,0:T(8,128)(2,1)S(1)}, bf16[768,768]{1,0:T(8,128)(2,1)}, u32[]{:S(2)}) copy-start(bf16[768,768]{1,0:T(8,128)(2,1)} %all-gather.5.cloned.1.call-done) | copy-start | bytes 3538948
  203.8 4.0 %copy-start.44 = (f32[768,768]{1,0:T(8,128)S(1)}, f32[768,768]{1,0:T(8,128)}, u32[]{:S(2)}) copy-start(f32[768,768]{1,0:T(8,128)} %copy-done.43) | copy-start | bytes 7077892
  207.7 2.5 copy-start.13
  207.8 2.5 copy-start.15
  210.2 24.4 %copy-start.5 = (f32[8,64,384]{2,1,0:T(8,128)S(1)}, f32[8,64,384]{2,1,0:T(8,128)}, u32[]{:S(2)}) copy-start(f32[8,64,384]{2,1,0:T(8,128)} %copy-done.4) | copy-start | bytes 2359300
  234.7 0.7 copy-start.7
  235.4 0.7 copy-start.8
  251.2 13.9 %copy-start.2 = (bf16[4,192,768]{2,1,0:T(8,128)(2,1)S(1)}, bf16[4,192,768]{2,1,0:T(8,128)(2,1)}, u32[]{:S(2)}) copy-start(bf16[4,192,768]{2,1,0:T(8,128)(2,1)} %copy-done.1) | copy-start | bytes 3538948
  265.9 1.5 copy-start.20
  268.5 32.3 %copy-start.11 = (bf16[1,192,768]{2,1,0:T(8,128)(2,1)S(1)}, bf16[1,192,768]{2,1,0:T(8,128)(2,1)}, u32[]{:S(2)}) copy-start(bf16[1,192,768]{2,1,0:T(8,128)(2,1)} %param.16) | copy-start | bytes 884740
  268.5 32.3 %copy-start.23 = (f32[768]{0:T(1024)S(1)}, f32[768]{0:T(1024)}, u32[]{:S(2)}) copy-start(f32[768]{0:T(1024)} %param.17) | copy-start | bytes 9220
  268.6 32.3 %copy-start.25 = (f32[192]{0:T(256)S(1)}, f32[192]{0:T(256)}, u32[]{:S(2)}) copy-start(f32[192]{0:T(256)} %copy-done.24) | copy-start | bytes 2308
  268.6 32.3 %copy-start.28 = (f32[192]{0:T(256)S(1)}, f32[192]{0:T(256)}, u32[]{:S(2)}) copy-start(f32[192]{0:T(256)} %copy-done.27) | copy-start | bytes 2308
  301.3 0.7 copy-start.26
  301.3 0.7 copy-start.32
  301.3 0.8 copy-start.30
  301.3 0.8 copy-start.29
  301.3 0.8 copy-start.31
  301.4 0.8 copy-start.36
  301.4 14.7 %copy-start.14 = (f32[192,768]{1,0:T(8,128)S(1)}, f32[192,768]{1,0:T(8,128)}, u32[]{:S(2)}) copy-start(f32[192,768]{1,0:T(8,128)} %copy-done.12) | copy-start | bytes 1769476
  374.4 4.4 %copy-start.17 = (bf16[768,768]{1,0:T(8,128)(2,1)S(1)}, bf16[768,768]{1,0:T(8,128)(2,1)}, u32[]{:S(2)}) copy-start(bf16[768,768]{1,0:T(8,128)(2,1)} %get-tuple-element.47) | copy-start | bytes 3538948
  378.8 1.7 copy-start.16
Sparse Core Ops, SparseCore 0:
  36.7 29.2 all-gather.2
  85.2 36.4 all-gather.4
  165.1 33.2 reduce-scatter.2
  203.7 34.2 reduce-scatter.4
  301.5 72.7 all-reduce.3

commit v2 on v1

--- a/solution.py
+++ b/solution.py
@@ -475,6 +475,514 @@
         + [DMA((size,)) for size in sizes for _ in range(2)],
         compiler_params=remote_params(collective_id),
     )(rows[None])
+
+
+class PlaneSum:
+    slots = 7
+
+    def __init__(self, u, o, bufs, send, recv):
+        self.u, self.o, self.send, self.recv = u, o, send, recv
+        self.rc, self.s1, self.ra, self.rb, self.sa, self.sb, self.ta, self.tb = bufs
+        ctx, self.x = lax.axis_index("context"), lax.axis_index("dp")
+        self.core, self.y = lax.rem(ctx, 2), lax.div(ctx, 2)
+        self.chip_peer = {"context": ctx + 1 - 2 * self.core}
+        self.y_peer = {"context": lax.rem(ctx + 2, 4)}
+        self.x_peer = {"dp": 1 - self.x}
+
+    @staticmethod
+    def scratch(shape, dtype):
+        tail = tuple(shape[1:])
+        return [pltpu.VMEM((count,) + tail, dtype) for count in (8, 8, 2, 2, 2, 2, 1, 1)] + [
+            DMA((10,)),
+            DMA((10,)),
+        ]
+
+    @staticmethod
+    def greet(bar):
+        ctx, x = lax.axis_index("context"), lax.axis_index("dp")
+        for peer in (
+            {"context": ctx + 1 - 2 * lax.rem(ctx, 2)},
+            {"context": lax.rem(ctx + 2, 4)},
+            {"dp": 1 - x},
+        ):
+            pl.semaphore_signal(bar, inc=1, device_id=peer, device_id_type=MESH)
+        return 3
+
+    def copy(self, at, src, dst, peer):
+        return pltpu.make_async_remote_copy(
+            src_ref=src,
+            dst_ref=dst,
+            send_sem=self.send.at[at],
+            recv_sem=self.recv.at[at],
+            device_id=peer,
+            device_id_type=MESH,
+        )
+
+    def got(self, at, ref):
+        pltpu.make_async_copy(ref, ref, self.recv.at[at]).wait()
+
+    def add(self, out, left, right):
+        f32 = jnp.float32
+        out[...] = (left[...].astype(f32) + right[...].astype(f32)).astype(out.dtype)
+
+    def hop(self, at):
+        x, y, core = self.x, self.y, self.core
+        o = self.o
+        mine_a, mine_b = core * 8 + 2 * x + y, core * 8 + 4 + 2 * y + x
+        pair_a, pair_b = pl.ds(core * 8 + 2 * x, 2), pl.ds(core * 8 + 4 + 2 * y, 2)
+        all_mine = pl.ds(core * 8, 8)
+        one = lambda at: pl.ds(at, 1)
+        return [
+            lambda: self.copy(0, self.u.at[pl.ds(8 - core * 8, 8)], self.rc, self.chip_peer),
+            lambda: self.copy(1, self.s1.at[pl.ds(2 - 2 * x, 2)], self.ra, self.x_peer),
+            lambda: self.copy(2, self.s1.at[pl.ds(6 - 2 * y, 2)], self.rb, self.y_peer),
+            lambda: self.copy(3, self.sa.at[one(1 - y)], self.ta, self.y_peer),
+            lambda: self.copy(4, self.sb.at[one(1 - x)], self.tb, self.x_peer),
+            lambda: self.copy(5, o.at[one(mine_a)], o.at[one(mine_a)], self.y_peer),
+            lambda: self.copy(6, o.at[one(mine_b)], o.at[one(mine_b)], self.x_peer),
+            lambda: self.copy(7, o.at[pair_a], o.at[pair_a], self.x_peer),
+            lambda: self.copy(8, o.at[pair_b], o.at[pair_b], self.y_peer),
+            lambda: self.copy(9, o.at[all_mine], o.at[all_mine], self.chip_peer),
+        ][at]()
+
+    def begin(self):
+        self.hop(0).start()
+
+    def first(self):
+        self.got(0, self.rc)
+        self.add(self.s1, self.u.at[pl.ds(self.core * 8, 8)], self.rc)
+        self.hop(1).start()
+        self.hop(2).start()
+
+    def second(self):
+        self.got(1, self.ra)
+        self.add(self.sa, self.s1.at[pl.ds(2 * self.x, 2)], self.ra)
+        self.hop(3).start()
+        self.got(2, self.rb)
+        self.add(self.sb, self.s1.at[pl.ds(4 + 2 * self.y, 2)], self.rb)
+        self.hop(4).start()
+
+    def third(self, out_a, out_b):
+        self.got(3, self.ta)
+        self.add(out_a, self.sa.at[pl.ds(self.y, 1)], self.ta)
+        self.got(4, self.tb)
+        self.add(out_b, self.sb.at[pl.ds(self.x, 1)], self.tb)
+
+    def own(self):
+        return (
+            self.o.at[pl.ds(self.core * 8 + 2 * self.x + self.y, 1)],
+            self.o.at[pl.ds(self.core * 8 + 4 + 2 * self.y + self.x, 1)],
+        )
+
+    def spread1(self):
+        self.hop(5).start()
+        self.hop(6).start()
+
+    def spread2(self):
+        x, y, core = self.x, self.y, self.core
+        self.got(5, self.o.at[pl.ds(core * 8 + 2 * x + 1 - y, 1)])
+        self.hop(7).start()
+        self.got(6, self.o.at[pl.ds(core * 8 + 4 + 2 * y + 1 - x, 1)])
+        self.hop(8).start()
+
+    def spread3(self):
+        x, y, core = self.x, self.y, self.core
+        self.got(7, self.o.at[pl.ds(core * 8 + 2 - 2 * x, 2)])
+        self.got(8, self.o.at[pl.ds(core * 8 + 6 - 2 * y, 2)])
+        self.hop(9).start()
+
+    def finish(self, which=range(10)):
+        if 9 in which:
+            self.got(9, self.o.at[pl.ds(8 - self.core * 8, 8)])
+        for at in which:
+            self.hop(at).wait_send()
+
+
+def line_greet(bar, me, n):
+    @pl.when(me > 0)
+    def _():
+        pl.semaphore_signal(bar, inc=1, device_id={"tensor": me - 1}, device_id_type=MESH)
+
+    @pl.when(me < n - 1)
+    def _():
+        pl.semaphore_signal(bar, inc=1, device_id={"tensor": me + 1}, device_id_type=MESH)
+
+    return jnp.where(me > 0, 1, 0) + jnp.where(me < n - 1, 1, 0)
+
+
+class LineScatter:
+    def __init__(self, n, x, o, buf, tmp, send, recv):
+        self.n, self.x, self.o, self.buf, self.tmp, self.send, self.recv = n, x, o, buf, tmp, send, recv
+        self.me = lax.axis_index("tensor")
+
+    @staticmethod
+    def scratch(n, own, cols, dtype):
+        return [
+            pltpu.VMEM((2, n - 1, own, cols), dtype),
+            pltpu.VMEM((2, n - 1, own, cols), dtype),
+            DMA((2, n - 1)),
+            DMA((2, n - 1)),
+        ]
+
+    def term(self, d, k):
+        return self.n - 1 - k if d == 0 else k
+
+    def sends(self, d, k):
+        return self.me < self.n - 1 - k if d == 0 else self.me > k
+
+    def behind(self, d):
+        return self.me > 0 if d == 0 else self.me < self.n - 1
+
+    def copy(self, d, k, first):
+        return pltpu.make_async_remote_copy(
+            src_ref=self.x.at[self.term(d, k)] if first else self.tmp.at[d, k],
+            dst_ref=self.buf.at[d, k],
+            send_sem=self.send.at[d, k],
+            recv_sem=self.recv.at[d, k],
+            device_id={"tensor": jnp.clip(self.me + 1 if d == 0 else self.me - 1, 0, self.n - 1)},
+            device_id_type=MESH,
+        )
+
+    def landed(self, d, k):
+        return pltpu.make_async_copy(self.buf.at[d, k], self.buf.at[d, k], self.recv.at[d, k])
+
+    def begin(self):
+        for d in range(2):
+
+            @pl.when(jnp.logical_not(self.behind(d)))
+            def _():
+                for k in range(self.n - 1):
+                    self.copy(d, k, True).start()
+
+    def step(self, k):
+        for d in range(2):
+
+            @pl.when(self.behind(d) & self.sends(d, k))
+            def _():
+                self.landed(d, k).wait()
+                at = self.term(d, k)
+                both = self.buf[d, k].astype(jnp.float32) + self.x[at].astype(jnp.float32)
+                self.tmp[d, k] = both.astype(self.tmp.dtype)
+                self.copy(d, k, False).start()
+
+    def end(self):
+        self.o[...] = self.x[self.me].astype(jnp.float32)
+        for d in range(2):
+            for k in range(self.n - 1):
+
+                @pl.when(self.behind(d) & (self.me == self.term(d, k)))
+                def _():
+                    self.landed(d, k).wait()
+                    self.o[...] += self.buf[d, k].astype(jnp.float32)
+
+        for d in range(2):
+            for k in range(self.n - 1):
+
+                @pl.when(self.sends(d, k))
+                def _():
+                    self.copy(d, k, False).wait_send()
+
+
+def scatter_and_sum_kernel(n, count, x_ref, *rest):
+    us, rest = rest[:count], rest[count:]
+    o_ref, outs, rest = rest[0], rest[1 : 1 + count], rest[1 + count :]
+    line = LineScatter(n, x_ref, o_ref, *rest[:4])
+    rest = rest[4:]
+    sums = [
+        PlaneSum(us[i], outs[i], rest[10 * i : 10 * i + 8], rest[10 * i + 8], rest[10 * i + 9])
+        for i in range(count)
+    ]
+    bar = pltpu.get_barrier_semaphore()
+    met = line_greet(bar, line.me, n) + PlaneSum.greet(bar)
+    pl.semaphore_wait(bar, met)
+    line.begin()
+    for item in sums:
+        item.begin()
+    for item in sums:
+        item.first()
+    line.step(0)
+    for item in sums:
+        item.second()
+    for k in range(1, n - 1):
+        line.step(k)
+    for item in sums:
+        item.third(*item.own())
+        item.spread1()
+    for item in sums:
+        item.spread2()
+    line.end()
+    for item in sums:
+        item.spread3()
+    for item in sums:
+        item.finish()
+
+
+def scatter_and_sum(x, units, n, collective_id):
+    rows, cols = x.shape
+    own = rows // n
+    result = pl.pallas_call(
+        functools.partial(scatter_and_sum_kernel, n, len(units)),
+        out_shape=(jax.ShapeDtypeStruct((own, cols), jnp.float32),)
+        + tuple(jax.ShapeDtypeStruct(unit.shape, unit.dtype) for unit in units),
+        in_specs=[VM] * (1 + len(units)),
+        out_specs=(VM,) * (1 + len(units)),
+        scratch_shapes=LineScatter.scratch(n, own, cols, x.dtype)
+        + [item for unit in units for item in PlaneSum.scratch(unit.shape, unit.dtype)],
+        compiler_params=remote_params(collective_id),
+    )(x.reshape(n, own, cols), *units)
+    return result[0], result[1:]
+
+
+def rows_back_sum_kernel(nc, nt, heads, x_ref, u_ref, o_ref, a_ref, send, recv, loc, za, zb, pa, pb, zsend, zrecv, *rest):
+    total = nc * nt
+    my_ctx, my_ten = lax.axis_index("context"), lax.axis_index("tensor")
+    me = my_ctx * nt + my_ten
+    bar = pltpu.get_barrier_semaphore()
+    for shift in range(1, total):
+        other = lax.rem(me + shift, total)
+        pl.semaphore_signal(bar, inc=1, device_id=spread(other, AXES, (nc, nt)), device_id_type=MESH)
+    x = lax.axis_index("dp")
+    pl.semaphore_signal(bar, inc=1, device_id={"dp": 1 - x}, device_id_type=MESH)
+    pl.semaphore_wait(bar, total)
+
+    unit = PlaneSum(u_ref, a_ref, rest[:8], rest[8], rest[9])
+
+    def copy(shift):
+        other = lax.rem(me + shift, total)
+        ctx, ten = lax.div(other, nt), lax.rem(other, nt)
+        return ctx < heads, pltpu.make_async_remote_copy(
+            src_ref=x_ref.at[ten * heads + jnp.minimum(ctx, heads - 1)],
+            dst_ref=o_ref.at[me],
+            send_sem=send.at[shift],
+            recv_sem=recv.at[shift],
+            device_id={"context": ctx, "tensor": ten},
+            device_id_type=MESH,
+        )
+
+    for shift in range(1, total):
+        goes, item = copy(shift)
+
+        @pl.when(goes)
+        def _():
+            item.start()
+
+    unit.begin()
+    own = pltpu.make_async_copy(
+        x_ref.at[my_ten * heads + jnp.minimum(my_ctx, heads - 1)], o_ref.at[me], loc
+    )
+    own.start()
+    own.wait()
+    unit.first()
+    unit.second()
+    unit.third(pa, pb)
+
+    def across(half, shift):
+        other = lax.rem(my_ten + shift, nt)
+        part, land = ((pa, za), (pb, zb))[half]
+        return pltpu.make_async_remote_copy(
+            src_ref=part.at[0, other],
+            dst_ref=land.at[my_ten],
+            send_sem=zsend.at[half, shift],
+            recv_sem=zrecv.at[half, shift],
+            device_id={"tensor": other},
+            device_id_type=MESH,
+        )
+
+    for half in range(2):
+        for shift in range(1, nt):
+            across(half, shift).start()
+    for half, (part, land, done) in enumerate(zip((pa, pb), (za, zb), unit.own())):
+        land[my_ten] = part[0, my_ten]
+        for shift in range(1, nt):
+            source = lax.rem(my_ten + nt - shift, nt)
+            pltpu.make_async_copy(land.at[source], land.at[source], zrecv.at[half, shift]).wait()
+        value = land[0].astype(jnp.float32)
+        for at in range(1, nt):
+            value = value + land[at].astype(jnp.float32)
+        done[0] = value.astype(done.dtype)
+    unit.spread1()
+    unit.spread2()
+
+    @pl.when(my_ctx < heads)
+    def _():
+        for shift in range(1, total):
+            source = lax.rem(me + total - shift, total)
+            pltpu.make_async_copy(o_ref.at[source], o_ref.at[source], recv.at[shift]).wait()
+
+    unit.spread3()
+    unit.finish()
+    for half in range(2):
+        for shift in range(1, nt):
+            across(half, shift).wait_send()
+    for shift in range(1, total):
+        goes, item = copy(shift)
+
+        @pl.when(goes)
+        def _():
+            item.wait_send()
+
+
+def rows_back_sum(x, unit, nc, nt, heads, collective_id):
+    total = nc * nt
+    piece = unit.shape[2:]
+    low = unit.dtype
+    return pl.pallas_call(
+        functools.partial(rows_back_sum_kernel, nc, nt, heads),
+        out_shape=(
+            jax.ShapeDtypeStruct((total,) + x.shape[1:], x.dtype),
+            jax.ShapeDtypeStruct((16,) + piece, low),
+        ),
+        in_specs=[VM, VM],
+        out_specs=(VM, VM),
+        scratch_shapes=[
+            DMA((total,)),
+            DMA((total,)),
+            DMA,
+            pltpu.VMEM((nt,) + piece, low),
+            pltpu.VMEM((nt,) + piece, low),
+            pltpu.VMEM((1, nt) + piece, low),
+            pltpu.VMEM((1, nt) + piece, low),
+            DMA((2, nt)),
+            DMA((2, nt)),
+        ]
+        + PlaneSum.scratch(unit.shape, low),
+        compiler_params=remote_params(collective_id),
+    )(x, unit)
+
+
+class LineGather:
+    def __init__(self, n, x, o, send, recv):
+        self.n, self.x, self.o, self.send, self.recv = n, x, o, send, recv
+        self.me = lax.axis_index("tensor")
+
+    def copy(self, d, s):
+        me, n = self.me, self.n
+        shard = jnp.clip(me - s if d == 0 else me + s, 0, n - 1)
+        return pltpu.make_async_remote_copy(
+            src_ref=self.x if s == 0 else self.o.at[shard],
+            dst_ref=self.o.at[shard],
+            send_sem=self.send.at[d, s],
+            recv_sem=self.recv.at[d, s],
+            device_id={"tensor": jnp.clip(me + 1 if d == 0 else me - 1, 0, n - 1)},
+            device_id_type=MESH,
+        )
+
+    def sends(self, d, s):
+        me, n = self.me, self.n
+        return (me - s >= 0) & (me < n - 1) if d == 0 else (me + s < n) & (me > 0)
+
+    def wait(self, d, s):
+        me, n = self.me, self.n
+
+        @pl.when(me - 1 - s >= 0 if d == 0 else me + 1 + s < n)
+        def _():
+            shard = jnp.clip(me - 1 - s if d == 0 else me + 1 + s, 0, n - 1)
+            pltpu.make_async_copy(self.o.at[shard], self.o.at[shard], self.recv.at[d, s]).wait()
+
+    def step(self, s):
+        for d in range(2):
+            if s > 0:
+                self.wait(d, s - 1)
+
+            @pl.when(self.sends(d, s))
+            def _():
+                self.copy(d, s).start()
+
+    def last(self):
+        for d in range(2):
+            self.wait(d, self.n - 2)
+
+    def finish(self):
+        for d in range(2):
+            for s in range(self.n - 1):
+
+                @pl.when(self.sends(d, s))
+                def _():
+                    self.copy(d, s).wait_send()
+
+
+def gather_pieces_kernel(n, x_ref, w_ref, o_ref, f_ref, held, s1, r1, s2, r2, s3, r3, loc):
+    me, ctx, x = lax.axis_index("tensor"), lax.axis_index("context"), lax.axis_index("dp")
+    place = ctx * 2 + x
+    bar = pltpu.get_barrier_semaphore()
+    met = line_greet(bar, me, n)
+    for shift in range(1, 8):
+        other = lax.rem(place + shift, 8)
+        pl.semaphore_signal(
+            bar, inc=1, device_id={"context": lax.div(other, 2), "dp": lax.rem(other, 2)}, device_id_type=MESH
+        )
+    pl.semaphore_wait(bar, met + 7)
+    small = LineGather(n, w_ref, held, s1, r1)
+    large = LineGather(n, x_ref, o_ref, s2, r2)
+    small.step(0)
+    large.step(0)
+    own = pltpu.make_async_copy(x_ref, o_ref.at[me], loc.at[0])
+    own.start()
+    piece = pltpu.make_async_copy(w_ref, held.at[me], loc.at[1])
+    piece.start()
+    piece.wait()
+    for s in range(1, n - 1):
+        small.step(s)
+    small.last()
+
+    def there(at):
+        ctx_, x_ = lax.div(at, 2), lax.rem(at, 2)
+        rows = pl.ds(pl.multiple_of((lax.div(ctx_, 2) * 2 + x_) * w_ref.shape[0], 16), w_ref.shape[0])
+        cols = pl.ds(pl.multiple_of(lax.rem(ctx_, 2) * w_ref.shape[1], 128), w_ref.shape[1])
+        return f_ref.at[:, rows, cols]
+
+    def push(shift):
+        other = lax.rem(place + shift, 8)
+        return pltpu.make_async_remote_copy(
+            src_ref=held,
+            dst_ref=there(place),
+            send_sem=s3.at[shift],
+            recv_sem=r3.at[shift],
+            device_id={"context": lax.div(other, 2), "dp": lax.rem(other, 2)},
+            device_id_type=MESH,
+        )
+
+    for shift in range(1, 8):
+        push(shift).start()
+    kept = pltpu.make_async_copy(held, there(place), loc.at[2])
+    kept.start()
+    for s in range(1, n - 1):
+        large.step(s)
+    large.last()
+    for shift in range(1, 8):
+        source = there(lax.rem(place + 8 - shift, 8))
+        pltpu.make_async_copy(source, source, r3.at[shift]).wait()
+    kept.wait()
+    own.wait()
+    small.finish()
+    large.finish()
+    for shift in range(1, 8):
+        push(shift).wait_send()
+
+
+def gather_pieces(x, w, n, collective_id):
+    rows, cols = x.shape
+    wide, deep = w.shape
+    ctx, dp = lax.axis_index("context"), lax.axis_index("dp")
+    piece = lax.dynamic_slice(
+        w,
+        ((lax.div(ctx, 2) * 2 + dp) * (wide // 4), lax.rem(ctx, 2) * (deep // 2)),
+        (wide // 4, deep // 2),
+    )
+    full, weight = pl.pallas_call(
+        functools.partial(gather_pieces_kernel, n),
+        out_shape=(
+            jax.ShapeDtypeStruct((n, rows, cols), x.dtype),
+            jax.ShapeDtypeStruct((n, wide, deep), w.dtype),
+        ),
+        in_specs=[VM, VM],
+        out_specs=(VM, VM),
+        scratch_shapes=[pltpu.VMEM((n,) + piece.shape, w.dtype)]
+        + [DMA((2, n - 1)) for _ in range(4)]
+        + [DMA((8,)), DMA((8,)), DMA((3,))],
+        compiler_params=remote_params(collective_id),
+    )(x, piece)
+    return full.reshape(n * rows, cols), weight.reshape(n * wide, deep)
 
 
 def dot(left, right, dims):
@@ -706,10 +1214,14 @@
     grad_out = cotangent[0]
     normed1, scale1 = norm_parts(tokens_own)
     hidden1 = (normed1 * first_gain + first_shift).astype(low)
-    hidden1_full = gather_rows(hidden1, nt, 0)
-
-    attend_full = lax.all_gather(after(attend_weight, hidden1_full), "tensor", axis=0, tiled=True)
-    grad_full = lax.all_gather(after(grad_out, attend_full), "tensor", axis=0, tiled=True)
+    square = nc == 4 and mesh_sizes["dp"] == 2
+    plane = ("context", "dp")
+    if square:
+        hidden1_full, attend_full = gather_pieces(hidden1, attend_weight, nt, 0)
+    else:
+        hidden1_full = gather_rows(hidden1, nt, 0)
+        attend_full = lax.all_gather(attend_weight, "tensor", axis=0, tiled=True)
+    grad_full = lax.all_gather(after(grad_out, hidden1_full), "tensor", axis=0, tiled=True)
 
     by_head = project_weight.reshape(3, width, heads, HEAD_DIM)
     bias = jnp.stack([project_bias[0], jnp.zeros_like(project_bias[0]), project_bias[1]])
@@ -728,19 +1240,21 @@
     activ = gelu_tanh(pre_act).astype(low)
     grad_act = dot(grad_full, shrink_weight, ((1,), (1,)))
     grad_pre = jax.vjp(gelu_tanh, pre_act)[1](grad_act)[0].astype(low)
-    grad_hidden2 = scatter_rows(dot(grad_pre, expand_weight, ((1,), (1,))).astype(low), nt, 4)
-
-    feed = jnp.dot(activ, shrink_weight, preferred_element_type=jnp.float32).astype(low)
-    feed_sum = lax.psum_scatter(
-        after(feed, grad_hidden2), "tensor", scatter_dimension=0, tiled=True
-    ).astype(jnp.float32)
-    outputs = (middle + feed_sum + shrink_bias).astype(low)[None]
-
     grad_shrink = cross_rows(activ, grad_full).astype(low)
     grad_expand = cross_rows(hidden2_full, grad_pre).astype(low)
+    grad_hidden2 = dot(grad_pre, expand_weight, ((1,), (1,))).astype(low)
+    if square:
+        units = [item.reshape((16, -1) + item.shape[1:]) for item in (grad_shrink, grad_expand)]
+        grad_hidden2, units = scatter_and_sum(grad_hidden2, units, nt, 4)
+        grad_shrink, grad_expand = (
+            unit.reshape(item.shape) for unit, item in zip(units, (grad_shrink, grad_expand))
+        )
+    else:
+        grad_hidden2 = scatter_rows(grad_hidden2, nt, 4)
+        grad_shrink, grad_expand = lax.psum((grad_shrink, grad_expand), plane)
     grad_expand_bias = jnp.sum(grad_pre.astype(jnp.float32), axis=0)
     grad_shrink_bias = jnp.sum(grad_out.astype(jnp.float32), axis=0)
-    grad_shrink, grad_expand = lax.psum((grad_shrink, grad_expand), ("context", "dp"))
+    feed = jnp.dot(activ, shrink_weight, preferred_element_type=jnp.float32).astype(low)
 
     grad_second_gain = jnp.sum(grad_hidden2 * normed2, axis=0)
     grad_second_shift = jnp.sum(grad_hidden2, axis=0)
@@ -750,18 +1264,32 @@
     grad_middle_low = grad_middle.astype(low)
     grad_attend_bias = jnp.sum(grad_middle_low.astype(jnp.float32), axis=0)
     grad_attended = dot(attend_full, grad_middle_low, ((1,), (1,))).astype(low)
-    grad_heads = rows_back(
-        grad_attended.reshape(nt * heads, HEAD_DIM, own_rows), nc, nt, heads, 5
-    )
     grad_attend = jnp.dot(attended, grad_middle_low, preferred_element_type=jnp.float32).astype(low)
-    grad_attend = lax.psum_scatter(grad_attend, "tensor", scatter_dimension=0, tiled=True)
-    grad_attend = lax.psum(grad_attend, ("context", "dp"))
+    grad_attended = grad_attended.reshape(nt * heads, HEAD_DIM, own_rows)
+    if square:
+        unit = grad_attend.reshape(nt, 16, -1, width).transpose(1, 0, 2, 3)
+        grad_heads, grad_attend = rows_back_sum(grad_attended, unit, nc, nt, heads, 5)
+        grad_attend = grad_attend.reshape(local_width, width)
+    else:
+        grad_heads = rows_back(grad_attended, nc, nt, heads, 5)
+        grad_attend = lax.psum_scatter(grad_attend, "tensor", scatter_dimension=0, tiled=True)
+        grad_attend = lax.psum(grad_attend, plane)
+
+    feed_sum = lax.psum_scatter(after(feed, grad_heads), "tensor", scatter_dimension=0, tiled=True)
 
     grad_qkv = attend_backward(qkv, tables, attended_full, lse, grad_heads, half)
     grad_rows = from_heads(grad_qkv, nc, heads, 6).reshape(3 * local_width, block_rows)
-    grad_hidden1 = scatter_rows(cross_rows(grad_rows, weight_rows).astype(low), nt, 7)
     grad_project = dot(hidden1_full, grad_rows, ((0,), (1,))).astype(low)
-    grad_project = lax.psum(grad_project, ("context", "dp"))
+    grad_hidden1 = cross_rows(grad_rows, weight_rows).astype(low)
+    if square:
+        unit = grad_project.reshape(16, -1, 3 * local_width)
+        grad_hidden1, (unit,) = scatter_and_sum(grad_hidden1, [unit], nt, 7)
+        grad_project = unit.reshape(grad_project.shape)
+    else:
+        grad_hidden1 = scatter_rows(grad_hidden1, nt, 7)
+        grad_project = lax.psum(grad_project, plane)
+    feed_sum = after(feed_sum, grad_hidden1).astype(jnp.float32)
+    outputs = (middle + feed_sum + shrink_bias).astype(low)[None]
     grad_project = (
         grad_project.reshape(width, heads, 3, HEAD_DIM).transpose(2, 0, 1, 3).reshape(3, width, local_width)
     )

time: 388 us -> 356 us (0.918)
  waiting for transfers between devices: 88.7 us -> 0.04 us
  Pallas kernels: 231 us -> 268 us
  local copies, waits for them, and re-layouts: 10.8 us -> 34.9 us
    pallas_call x3 -> x4, Pallas kernels: 80.9 us -> 159 us  [the longest x2 88.9 us: scatter_and_sum(): pl.pallas_call(functools.partial(scatter_and_sum_kernel, n, len(units)),...]
    psum x1 -> x0, waiting for transfers between devices: 57.3 us -> none  [per_device(): grad_project = lax.psum(grad_project, ('context', 'dp'))]
    pallas_call x2 -> x1, Pallas kernels: 65.3 us -> 20.8 us  [gather_rows(): pl.pallas_call(functools.partial(gather_kernel, n), out_shape=jax.ShapeDt...]
    reduce_scatter x2 -> x1, waiting for transfers between devices: 31.3 us -> 0.01 us  [per_device(): lax.psum_scatter(after(feed, grad_heads), 'tensor', scatter_dimension=0,...]
    convert_element_type x1 -> x3, local copies, waits for them, and re-layouts: 0.98 us -> 10.3 us  [per_device(): f32 = lambda value: value.astype(jnp.float32)]
    reshape x0 -> x2, local copies, waits for them, and re-layouts: none -> 4.71 us  [per_device(): unit = grad_attend.reshape(nt, 16, -1, width).transpose(1, 0, 2, 3)]
    convert_element_type x4 -> x2, other arithmetic: 7.58 us -> 3.3 us  [per_device(): f32 = lambda value: value.astype(jnp.float32)]
    unnamed x102 -> x134, local copies, waits for them, and re-layouts: 6.74 us -> 8.97 us
  transfers between devices with their start and end apart: 5 -> 2, of which waited for: 2 -> 0; matrix products, arithmetic and copies ran while one was open for 7% -> 10% of each run, Pallas kernels for 46% -> 36%
where the time goes in v2:
time: 356 us
  Pallas kernels  268 us (75%)
  local copies, waits for them, and re-layouts  34.9 us (10%)
  matrix products  21.5 us (6%)
  other arithmetic  16.3 us (5%)
  between operations  14.9 us (4%)
    pallas_call x2, Pallas kernels, scatter_and_sum(): pl.pallas_call(functools.partial(scatter_and_sum_kernel, n, len(units)),...  88.9 us
    pallas_call x1, Pallas kernels, rows_back_sum(): pl.pallas_call(functools.partial(rows_back_sum_kernel, nc, nt, heads), ou...  39.3 us
    pallas_call x1, Pallas kernels, gather_pieces(): pl.pallas_call(functools.partial(gather_pieces_kernel, n), out_shape=(jax...  31.2 us
    pallas_call x1, Pallas kernels, gather_rows(): pl.pallas_call(functools.partial(gather_kernel, n), out_shape=jax.ShapeDt...  20.8 us
    pallas_call x1, Pallas kernels, to_rows(): pl.pallas_call(functools.partial(rows_kernel, nc, nt, heads), out_shape=j...  20.3 us
    pallas_call x1, Pallas kernels, attend_backward(): pl.pallas_call(functools.partial(backward_kernel, half), out_shape=jax.Sh...  15.2 us
    pallas_call x1, Pallas kernels, from_heads(): pl.pallas_call(functools.partial(from_heads_kernel, nc, heads), out_shape...  14.9 us
    pallas_call x1, Pallas kernels, sum_vectors(): pl.pallas_call(functools.partial(vectors_kernel, names, sizes, shared), o...  14.8 us
  transfers between devices with their start and end apart: 2, of which 0 were waited for; matrix products, arithmetic and copies ran while one was open for 10% of the time, Pallas kernels for 36%

profile of v2, /device:TPU:0, one launch (start us, length us, event | category | flops | bytes accessed | tf_op | source)
XLA Modules:
  0.0 355.6 jit_solution(12805180060533820287)
XLA Ops:
  7.3 1.2 convert_reduce_fusion.3
  8.5 1.2 fusion.23
  9.7 0.8 dynamic_slice.3.w_ref
  10.5 1.2 fusion.16.x_ref
  11.7 31.2 %shard_map.263 = (bf16[4,192,768]{2,1,0:T(8,128)(2,1)S(1)}, bf16[4,192,768]{2,1,0:T(8,128)(2,1)S(1)}) custom-call(bf16[192,768]{1,0:T(8,128)(2,1)S(1)} %fusion.16.x_ref, bf16[48,384]{1,0:T(8,128)(2,1)S(1)} %dynamic_slice.3.w_ref), custom_call_target="tpu_custom_call" | custom-call | tf_op jit(solution)/shard_map/pallas_call | solution.py:972
  43.1 0.8 fusion.31
  44.2 0.6 copy.67
  44.8 1.4 add.107
  46.1 0.8 select_reduce_fusion
  46.9 0.5 broadcast.142
  47.4 2.0 reduce.23
  49.4 1.3 reshape_squeeze.9
  50.7 1.4 fusion.30
  52.1 1.3 copy.62
  53.4 0.6 copy.63
  54.0 1.2 copy.53
  55.2 0.9 add_convert_fusion
  56.2 10.0 %shard_map.264.qkv_ref = bf16[4,192,768]{2,1,0:T(8,128)(2,1)S(1)} custom-call(bf16[3,192,768]{2,1,0:T(8,128)(2,1)S(1)} %bitcast.120), custom_call_target="tpu_custom_call" | custom-call | tf_op jit(solution)/shard_map/pallas_call | solution.py:254
  66.3 0.8 convert_reduce_fusion.6
  67.0 12.3 %shard_map.265 = (bf16[16,64,192]{2,1,0:T(8,128)(2,1)S(1)}, f32[8,64,384]{2,1,0:T(8,128)S(1)}, f32[8,1,384]{2,1,0:T(1,128)S(1)}) custom-call(s32[8]{0:T(128)S(1)} %get-tuple-element.74.slot_ref, s32[8]{0:T(128)S(1)} %get-tuple-element.62.low_ref, s32[1]{0:T(128)} %bitcast.3.on_ref, bf16[4,192,768]{2,1,0:T(8,128)(2,1)S(1)} %shard_map.264.qkv_ref, ...), custom_call_target="tpu_custom_call" | custom-call | tf_op jit(solution)/shard_map/pallas_call | solution.py:1057
  79.4 20.3 %shard_map.266 = bf16[12,64,192]{2,1,0:T(8,128)(2,1)S(1)} custom-call(bf16[16,64,192]{2,1,0:T(8,128)(2,1)S(1)} %get-tuple-element.30.x_ref), custom_call_target="tpu_custom_call" | custom-call | tf_op jit(solution)/shard_map/pallas_call | solution.py:355
  99.8 0.7 copy-done.1
  100.5 0.5 fusion.32
  101.1 0.2 multiply_reduce_fusion.2
  101.3 0.4 copy-done.36
  101.7 0.6 copy-done.41
  102.3 0.2 add_convert_fusion.2.x_ref
  102.5 20.8 %shard_map.267 = bf16[4,192,768]{2,1,0:T(8,128)(2,1)S(1)} custom-call(bf16[192,768]{1,0:T(8,128)(2,1)S(1)} %add_convert_fusion.2.x_ref), custom_call_target="tpu_custom_call" | custom-call | tf_op jit(solution)/shard_map/pallas_call | solution.py:96
  123.3 1.1 fusion.33
  124.4 1.4 copy-done.60
  125.8 2.7 convolution_convert_fusion.5
  128.5 5.0 %convert_reduce_fusion = (f32[768]{0:T(1024)}, bf16[768,768]{1,0:T(8,128)(2,1)S(1)}) fusion(f32[768,768]{1,0:T(8,128)} %copy-done.60, f32[768]{0:T(1024)} %param.26, bf16[768,768]{1,0:T(8,128)(2,1)} %all-gather.2.cloned.1.call-done, bf16[768,768]{1,0:T(8,128)(2,1)S(1)} %copy-done), kind=kOutput, calls=%fused_computation.9 | convolution fusion | flops 919534848 | bytes 5904384 | tf_op jit(solution)/shard_map/dot_general | solution.py:989
  133.5 2.1 convolution_convert_fusion.2
  135.6 1.1 convolution_convert_fusion.4
  136.9 0.8 copy-done.61
  137.7 1.4 convolution_convert_fusion.3
  139.2 37.4 %shard_map.268 = (f32[192,768]{1,0:T(8,128)S(1)}, bf16[16,48,768]{2,1,0:T(8,128)(2,1)S(1)}, bf16[16,48,768]{2,1,0:T(8,128)(2,1)S(1)}) custom-call(bf16[4,192,768]{2,1,0:T(8,128)(2,1)S(1)} %bitcast.115, bf16[16,48,768]{2,1,0:T(8,128)(2,1)S(1)} %bitcast.116, bf16[16,48,768]{2,1,0:T(8,128)(2,1)} %bitcast.126), custom_call_target="tpu_custom_call" | custom-call | tf_op jit(solution)/shard_map/pallas_call | solution.py:723
  176.6 1.1 multiply_reduce_fusion
  177.7 0.9 convert_reduce_fusion.4
  178.6 1.3 convolution_convert_fusion.7
  179.9 1.5 convolution_convert_fusion.1
  181.6 3.1 reshape.177
  184.7 1.6 copy.66
  186.3 39.3 %shard_map.269 = (bf16[16,64,192]{2,1,0:T(8,128)(2,1)S(1)}, bf16[16,12,768]{2,1,0:T(8,128)(2,1)S(1)}) custom-call(bf16[12,64,192]{2,1,0:T(8,128)(2,1)S(1)} %bitcast.114, bf16[16,4,12,768]{3,2,1,0:T(8,128)(2,1)S(1)} %bitcast.106), custom_call_target="tpu_custom_call" | custom-call | tf_op jit(solution)/shard_map/pallas_call | solution.py:829
  225.7 15.2 %shard_map.270.x_ref = bf16[4,192,768]{2,1,0:T(8,128)(2,1)S(1)} custom-call(s32[8]{0:T(128)S(1)} %get-tuple-element.74.slot_ref, s32[8]{0:T(128)S(1)} %copy-done.16, s32[1]{0:T(128)} %bitcast.3.on_ref, bf16[4,192,768]{2,1,0:T(8,128)(2,1)S(1)} %shard_map.264.qkv_ref, s32[8,1,384]{2,1,0:T(1,128)S(1)} %bitcast.122, f32[8,64,384]{2,1,0:T(8,128)S(1)} %copy-done.13, ...), custom_call_target="tpu_custom_call" | custom-call | tf_op jit(solution)/shard_map/pallas_call | solution.py:1123
  240.9 14.9 %shard_map.271 = bf16[3,192,768]{2,1,0:T(8,128)(2,1)S(1)} custom-call(bf16[4,192,768]{2,1,0:T(8,128)(2,1)S(1)} %shard_map.270.x_ref), custom_call_target="tpu_custom_call" | custom-call | tf_op jit(solution)/shard_map/pallas_call | solution.py:301
  255.8 0.2 convert_reduce_fusion.1
  256.0 1.8 convolution_convert_fusion.6
  257.8 2.1 convolution_convert_fusion
  260.2 1.5 copy.57
  261.9 0.9 reshape.185
  262.8 1.3 copy-done.7
  264.0 51.5 %shard_map.272 = (f32[192,768]{1,0:T(8,128)S(1)}, bf16[16,48,576]{2,1,0:T(8,128)(2,1)S(1)}) custom-call(bf16[4,192,768]{2,1,0:T(8,128)(2,1)S(1)} %bitcast.117, bf16[16,48,576]{2,1,0:T(8,128)(2,1)S(1)} %bitcast.109), custom_call_target="tpu_custom_call" | custom-call | tf_op jit(solution)/shard_map/pallas_call | solution.py:723
  315.6 0.9 copy-done.10
  316.5 0.4 fusion.22
  317.1 14.8 %shard_map.273 = f32[8,768]{1,0:T(8,128)S(1)} custom-call(f32[1,8,768]{2,1,0:T(8,128)S(1)} %broadcast_in_dim_reshape.3.x_ref), custom_call_target="tpu_custom_call" | custom-call | tf_op jit(solution)/shard_map/pallas_call | solution.py:468
  332.0 0.6 slice.73
  332.6 3.6 %reshape.189 = f32[768,3,3,64]{3,2,1,0:T(4,128)} reshape(bf16[16,48,576]{2,1,0:T(8,128)(2,1)S(1)} %copy-done.11) | data formatting | bytes 2654208 | tf_op jit(solution)/shard_map/convert_element_type | solution.py:1319
  336.2 5.8 %copy.61 = f32[768,3,3,64]{0,3,1,2:T(8,128)} copy(f32[768,3,3,64]{3,2,1,0:T(4,128)} %reshape.189) | data formatting | bytes 3538944 | tf_op jit(solution)/shard_map/convert_element_type | solution.py:1319
  342.1 0.7 slice_reduce_fusion
  342.7 1.0 fusion.25
  343.7 1.7 bitcast_convert_fusion.1
  345.3 1.7 bitcast_convert_fusion
  347.0 1.7 fusion.24
  (152 shorter events, 1.7 us)
Async XLA Ops:
  7.2 118.6 %copy-start = (bf16[768,768]{1,0:T(8,128)(2,1)S(1)}, bf16[768,768]{1,0:T(8,128)(2,1)}, u32[]{:S(2)}) copy-start(bf16[768,768]{1,0:T(8,128)(2,1)} %param.27) | copy-start | bytes 3538948
  7.2 35.8 %copy-start.30 = (s32[1,3072]{1,0:T(1,128)S(1)}, s32[1,3072]{1,0:T(1,128)}, u32[]{:S(2)}) copy-start(s32[1,3072]{1,0:T(1,128)} %param.29) | copy-start | bytes 36868
  7.2 121.3 %all-gather.2.cloned.1.call-start = ((), (), s32[]{:S(2)}) async-start(), calls=%async_computation.1 | async-start | bytes 1474560 | tf_op jit(solution)/shard_map/all_gather | solution.py:1224
  8.4 2.0 copy-start.34
  9.7 0.8 copy-start.39
  42.9 13.2 %copy-start.17 = (bf16[4,192,768]{2,1,0:T(8,128)(2,1)}, bf16[4,192,768]{2,1,0:T(8,128)(2,1)S(1)}, u32[]{:S(2)}) copy-start(bf16[4,192,768]{2,1,0:T(8,128)(2,1)S(1)} %get-tuple-element.29) | copy-start | bytes 3538948
  42.9 304.1 %reduce-scatter.2.cloned.1.call-start = ((), (), s32[]{:S(2)}) async-start(), calls=%async_computation.2 | async-start | bytes 1474560 | tf_op jit(solution)/shard_map/reduce_scatter | solution.py:1278
  54.0 1.3 copy-start.53
  55.2 1.0 copy-start.28
  56.2 10.1 %copy-start.47 = (s32[8,1]{0,1:T(1,128)S(1)}, s32[8,1]{0,1:T(1,128)}, u32[]{:S(2)}) copy-start(s32[8,1]{0,1:T(1,128)} %copy.62) | copy-start | bytes 100
  56.2 10.1 %copy-start.48 = (s32[8,1]{0,1:T(1,128)S(1)}, s32[8,1]{0,1:T(1,128)}, u32[]{:S(2)}) copy-start(s32[8,1]{0,1:T(1,128)} %copy.63) | copy-start | bytes 100
  56.2 10.1 %copy-start.54 = (s32[8]{0:T(128)S(1)}, s32[8]{0:T(128)}, u32[]{:S(2)}) copy-start(s32[8]{0:T(128)} %param.30) | copy-start | bytes 100
  56.2 44.3 %copy-start.22 = (bf16[1,192,768]{2,1,0:T(8,128)(2,1)S(1)}, bf16[1,192,768]{2,1,0:T(8,128)(2,1)}, u32[]{:S(2)}) copy-start(bf16[1,192,768]{2,1,0:T(8,128)(2,1)} %param.16) | copy-start | bytes 884740
  56.2 44.3 %copy-start.49 = (f32[768]{0:T(1024)S(1)}, f32[768]{0:T(1024)}, u32[]{:S(2)}) copy-start(f32[768]{0:T(1024)} %param.22) | copy-start | bytes 9220
  79.4 21.9 %copy-start.12 = (f32[8,64,384]{2,1,0:T(8,128)}, f32[8,64,384]{2,1,0:T(8,128)S(1)}, u32[]{:S(2)}) copy-start(f32[8,64,384]{2,1,0:T(8,128)S(1)} %get-tuple-element.36.full_ref) | copy-start | bytes 2359300
  79.4 21.9 %copy-start.14 = (f32[8,1,384]{2,1,0:T(1,128)}, f32[8,1,384]{2,1,0:T(1,128)S(1)}, u32[]{:S(2)}) copy-start(f32[8,1,384]{2,1,0:T(1,128)S(1)} %get-tuple-element.37.lse_ref) | copy-start | bytes 36868
  79.4 22.9 %copy-start.31 = (f32[768]{0:T(1024)S(1)}, f32[768]{0:T(1024)}, u32[]{:S(2)}) copy-start(f32[768]{0:T(1024)} %param.23) | copy-start | bytes 9220
  79.4 22.9 %copy-start.50 = (f32[768]{0:T(1024)S(1)}, f32[768]{0:T(1024)}, u32[]{:S(2)}) copy-start(f32[768]{0:T(1024)} %param.24) | copy-start | bytes 9220
  99.8 0.7 copy-start.1
  101.1 23.3 %copy-start.19 = (f32[192,768]{1,0:T(8,128)}, f32[192,768]{1,0:T(8,128)S(1)}, u32[]{:S(2)}) copy-start(f32[192,768]{1,0:T(8,128)S(1)} %get-tuple-element.73) | copy-start | bytes 1769476
  101.1 22.2 %copy-start.55 = (bf16[768,768]{1,0:T(8,128)(2,1)S(1)}, bf16[768,768]{1,0:T(8,128)(2,1)}, u32[]{:S(2)}) copy-start(bf16[768,768]{1,0:T(8,128)(2,1)} %param.25) | copy-start | bytes 3538948
  101.1 0.7 copy-start.36
  101.7 0.6 copy-start.41
  123.3 1.1 copy-start.8
  123.3 2.5 copy-start.58
  124.4 1.4 copy-start.60
  128.5 5.0 %copy-start.9 = (bf16[4,192,768]{2,1,0:T(8,128)(2,1)S(1)}, bf16[4,192,768]{2,1,0:T(8,128)(2,1)}, u32[]{:S(2)}) copy-start(bf16[4,192,768]{2,1,0:T(8,128)(2,1)} %copy-done.8) | copy-start | bytes 3538948
  133.5 2.1 copy-start.56
  135.6 1.3 copy-start.57
  135.6 1.3 copy-start.59
  135.6 2.0 copy-start.61
  139.1 37.5 %copy-start.20 = (f32[192,768]{1,0:T(8,128)S(1)}, f32[192,768]{1,0:T(8,128)}, u32[]{:S(2)}) copy-start(f32[192,768]{1,0:T(8,128)} %copy-done.19) | copy-start | bytes 1769476
  139.1 37.5 %copy-start.32 = (f32[768]{0:T(1024)S(1)}, f32[768]{0:T(1024)}, u32[]{:S(2)}) copy-start(f32[768]{0:T(1024)} %param.23) | copy-start | bytes 9220
  139.2 37.5 %copy-start.37 = (f32[192]{0:T(256)S(1)}, f32[192]{0:T(256)}, u32[]{:S(2)}) copy-start(f32[192]{0:T(256)} %copy-done.36) | copy-start | bytes 2308
  139.2 37.5 %copy-start.42 = (f32[192]{0:T(256)S(1)}, f32[192]{0:T(256)}, u32[]{:S(2)}) copy-start(f32[192]{0:T(256)} %copy-done.41) | copy-start | bytes 2308
  139.2 38.5 %copy-start.26 = (bf16[1,192,768]{2,1,0:T(8,128)(2,1)S(1)}, bf16[1,192,768]{2,1,0:T(8,128)(2,1)}, u32[]{:S(2)}) copy-start(bf16[1,192,768]{2,1,0:T(8,128)(2,1)} %param.31) | copy-start | bytes 884740
  176.6 3.3 copy-start.3
  176.6 3.3 copy-start.5
  177.7 2.2 copy-start.2
  178.6 1.3 copy-start.24
  179.9 1.5 copy-start.27
  186.3 39.3 %copy-start.13 = (f32[8,64,384]{2,1,0:T(8,128)S(1)}, f32[8,64,384]{2,1,0:T(8,128)}, u32[]{:S(2)}) copy-start(f32[8,64,384]{2,1,0:T(8,128)} %copy-done.12) | copy-start | bytes 2359300
  186.3 39.3 %copy-start.15 = (f32[8,1,384]{2,1,0:T(1,128)S(1)}, f32[8,1,384]{2,1,0:T(1,128)}, u32[]{:S(2)}) copy-start(f32[8,1,384]{2,1,0:T(1,128)} %copy-done.14) | copy-start | bytes 36868
  186.3 39.3 %copy-start.16 = (s32[8]{0:T(128)S(1)}, s32[8]{0:T(128)}, u32[]{:S(2)}) copy-start(s32[8]{0:T(128)} %get-tuple-element.61.high_ref) | copy-start | bytes 100
  240.9 15.2 %copy-start.18 = (bf16[4,192,768]{2,1,0:T(8,128)(2,1)S(1)}, bf16[4,192,768]{2,1,0:T(8,128)(2,1)}, u32[]{:S(2)}) copy-start(bf16[4,192,768]{2,1,0:T(8,128)(2,1)} %copy-done.17) | copy-start | bytes 3538948
  256.0 1.8 copy-start.29
  261.8 54.7 %copy-start.23 = (bf16[1,192,768]{2,1,0:T(8,128)(2,1)S(1)}, bf16[1,192,768]{2,1,0:T(8,128)(2,1)}, u32[]{:S(2)}) copy-start(bf16[1,192,768]{2,1,0:T(8,128)(2,1)} %param.16) | copy-start | bytes 884740
  261.8 54.7 %copy-start.33 = (f32[768]{0:T(1024)S(1)}, f32[768]{0:T(1024)}, u32[]{:S(2)}) copy-start(f32[768]{0:T(1024)} %param.17) | copy-start | bytes 9220
  261.8 54.7 %copy-start.35 = (f32[192]{0:T(256)S(1)}, f32[192]{0:T(256)}, u32[]{:S(2)}) copy-start(f32[192]{0:T(256)} %copy-done.34) | copy-start | bytes 2308
  261.8 54.7 %copy-start.40 = (f32[192]{0:T(256)S(1)}, f32[192]{0:T(256)}, u32[]{:S(2)}) copy-start(f32[192]{0:T(256)} %copy-done.39) | copy-start | bytes 2308
  261.8 55.1 %copy-start.38 = (f32[6144]{0:T(1024)S(1)}, f32[6144]{0:T(1024)}, u32[]{:S(2)}) copy-start(f32[6144]{0:T(1024)} %custom-call) | copy-start | bytes 73732
  261.8 55.1 %copy-start.46 = (f32[768]{0:T(1024)S(1)}, f32[768]{0:T(1024)}, u32[]{:S(2)}) copy-start(f32[768]{0:T(1024)} %get-tuple-element.65) | copy-start | bytes 9220
  261.9 55.1 %copy-start.44 = (f32[768]{0:T(1024)S(1)}, f32[768]{0:T(1024)}, u32[]{:S(2)}) copy-start(f32[768]{0:T(1024)} %get-tuple-element.44) | copy-start | bytes 9220
  261.9 55.1 %copy-start.43 = (f32[768]{0:T(1024)S(1)}, f32[768]{0:T(1024)}, u32[]{:S(2)}) copy-start(f32[768]{0:T(1024)} %get-tuple-element.50) | copy-start | bytes 9220
  261.9 55.1 %copy-start.45 = (f32[768]{0:T(1024)S(1)}, f32[768]{0:T(1024)}, u32[]{:S(2)}) copy-start(f32[768]{0:T(1024)} %get-tuple-element.67) | copy-start | bytes 9220
  261.9 55.1 %copy-start.52 = (f32[768]{0:T(1024)S(1)}, f32[768]{0:T(1024)}, u32[]{:S(2)}) copy-start(f32[768]{0:T(1024)} %get-tuple-element.63) | copy-start | bytes 9220
  262.8 1.3 copy-start.7
  315.6 0.9 copy-start.10
  316.5 16.1 %copy-start.11 = (bf16[16,48,576]{2,1,0:T(8,128)(2,1)S(1)}, bf16[16,48,576]{2,1,0:T(8,128)(2,1)}, u32[]{:S(2)}) copy-start(bf16[16,48,576]{2,1,0:T(8,128)(2,1)} %copy-done.10) | copy-start | bytes 2654212
  336.2 6.5 %copy-start.25 = (f32[192,768]{1,0:T(8,128)S(1)}, f32[192,768]{1,0:T(8,128)}, u32[]{:S(2)}) copy-start(f32[192,768]{1,0:T(8,128)} %copy-done.24) | copy-start | bytes 1769476
  342.1 1.6 copy-start.6
  343.7 1.7 copy-start.4
  345.3 1.7 copy-start.21
  345.3 1.7 copy-start.51
Sparse Core Ops, SparseCore 0:
  43.0 28.6 all-gather.1
  260.1 46.1 reduce-scatter.1
